TPU v7x, 128 devices: a whole 4x4x4 slice. The times are simulated.
128 devices in a mesh: sx: 16 (over x, y), sy: 8 (over z, core).
Axes of the slice: x: 4, y: 4, z: 4, core: 2. Of those that a mesh axis runs over, the one named last changes fastest.
Arguments:
- features: bfloat16 [512, 256, 256], P('sx', 'sy'), may hold values from -6 to 6
- coarse_features: bfloat16 [128, 256], P(('sx', 'sy')), may hold values from -6 to 6
- fine_index: int32 [32, 16, 128], P('sx', 'sy'), may hold values from 0 to 6399, as said below
- own_order: int32 [32, 16, 256], P('sx', 'sy'), may hold values from 0 to 255, each once within a row
Outputs:
- factor: float32 [32, 16, 512, 256], P('sx', 'sy')
Inputs may be any that keep to these rules, and one draw needn't show every extreme that they name: `fine_index`: the 128 entries of one supernode are distinct and each names a cell of the 80 by 80 window centred on its own block, outside that block (row f // 80, column f % 80 of the window).
All inputs are finite; a program needn't handle non-finite values.
Results may differ from a plain program's by a relative error of at most 0.0003.
Values may be sent and summed in bfloat16 or wider, within the bound.
A program may use at most 320 MiB of HBM per device.

v0:
```python
import jax
import jax.numpy as jnp
from jax import lax
from jax.sharding import PartitionSpec as P

SB = 16
REACH = 2


NUGGET_VALUE = 0.3


def padded_2(block, sides, width):
    for axis, dim in sides:
        count = lax.axis_size(axis)
        forward = [(i, i + 1) for i in range(count - 1)]
        forward.append((count - 1, 0))
        backward = [(target, source) for source, target in forward]
        low = lax.ppermute(
            lax.slice_in_dim(block, block.shape[dim] - width, None, axis=dim), axis, forward
        )
        high = lax.ppermute(lax.slice_in_dim(block, 0, width, axis=dim), axis, backward)
        block = jnp.concatenate([low, block, high], axis=dim)
    return block


def factor_blocks(point_set, own_count):
    gram = jnp.einsum("smd,snd->smn", point_set, point_set, preferred_element_type=jnp.float32)
    squares = jnp.diagonal(gram, axis1=1, axis2=2)
    feat_width = point_set.shape[2]
    total = point_set.shape[1]
    theta = jnp.exp(-(squares[:, :, None] + squares[:, None, :] - 2.0 * gram) / feat_width)
    theta = theta + NUGGET_VALUE * jnp.eye(total, dtype=jnp.float32)
    lower = jnp.linalg.cholesky(theta)
    target = jnp.concatenate(
        [
            jnp.zeros((total - own_count, own_count), jnp.float32),
            jnp.eye(own_count, dtype=jnp.float32),
        ],
        axis=0,
    )

    def solve_one(lower_one):
        return jax.scipy.linalg.solve_triangular(lower_one, target, lower=True, trans="T")

    return jax.vmap(solve_one)(lower)


def body(features, coarse_features, fine_index, own_order):
    block_x, block_y, fine_count = fine_index.shape
    own_count = own_order.shape[2]
    rim_width = REACH * SB
    coarse = lax.all_gather(coarse_features, ("sx", "sy"), axis=0, tiled=True)
    padded = padded_2(features, (("sx", 0), ("sy", 1)), rim_width)
    pad_width = padded.shape[1]
    feat_width = padded.shape[2]
    flat_rows = padded.reshape(-1, feat_width)
    win_side = (2 * REACH + 1) * SB
    start_x = (jnp.arange(block_x, dtype=jnp.int32) * SB)[:, None, None]
    start_y = (jnp.arange(block_y, dtype=jnp.int32) * SB)[None, :, None]
    fine_flat = (start_x + fine_index // win_side) * pad_width + start_y + fine_index % win_side
    own_flat = (
        (start_x + rim_width + own_order // SB) * pad_width + start_y + rim_width + own_order % SB
    )
    chosen = jnp.concatenate([fine_flat, own_flat], axis=2).reshape(
        block_x * block_y, fine_count + own_count
    )
    gathered = jnp.take(flat_rows, chosen, axis=0)
    block_count = chosen.shape[0]
    coarse_rows = jnp.broadcast_to(coarse[None], (block_count,) + coarse.shape)
    point_set = jnp.concatenate([coarse_rows, gathered], axis=1)
    factor = factor_blocks(point_set, own_count)
    return factor.reshape(block_x, block_y, factor.shape[1], factor.shape[2])


def solution(mesh):
    in_specs = (
        P("sx", "sy", None),
        P(("sx", "sy"), None),
        P("sx", "sy", None),
        P("sx", "sy", None),
    )
    out_specs = P("sx", "sy", None, None)
    return jax.shard_map(body, mesh=mesh, in_specs=in_specs, out_specs=out_specs, check_vma=False)
```

profile of v0, /device:TPU:1, one launch (start us, length us, event | category | flops | bytes accessed | tf_op | source)
XLA Modules:
  0.0 687.6 jit_solution(8523711429970733920)
XLA Ops:
  0.0 2.1 collective-permute-start
  2.1 3.6 collective-permute-start.1
  5.8 0.8 fusion.39
  6.5 0.8 fusion.40
  7.3 10.2 %collective-permute-done = bf16[32,32,256]{2,1,0:T(8,128)(2,1)S(1)} collective-permute-done((bf16[32,32,256]{2,1,0:T(8,128)(2,1)}, bf16[32,32,256]{2,1,0:T(8,128)(2,1)S(1)}, u32[]{:S(2)}, u32[]{:S(2)}) %collective-permute-start) | collective-permute-done | bytes 524320 | tf_op jit(solution)/shard_map/ppermute | solution.py:19
  17.6 0.8 constant_dynamic-update-slice_fusion.2
  18.4 1.9 constant_dynamic-update-slice_fusion.1
  20.3 0.8 constant_dynamic-update-slice_fusion
  21.1 2.8 collective-permute-start.2
  23.9 46.5 %all-gather = bf16[128,1,256]{2,1,0:T(2,128)(2,1)S(1)} all-gather(bf16[1,1,256]{2,1,0:T(2,128)(2,1)} %bitcast.73), channel_id=1, replica_groups=mesh['sx'=16,'sy'=8] {'sx','sy'}, dimensions={0}, use_global_device_ids=true | all-gather | bytes 66048 | tf_op jit(solution)/shard_map/all_gather | solution.py:53
  70.5 0.1 iota_compare_fusion.2
  70.6 0.2 fusion.18
  71.0 3.9 pad_maximum_fusion
  74.9 6.6 gather_fusion
  81.5 0.3 broadcast_select_fusion
  81.8 2.7 fusion.11
  84.4 60.3 %copy.59 = f32[4,512,512]{0,2,1:T(8,128)} copy(f32[4,512,512]{2,1,0:T(8,128)} %fusion.11) | data formatting | bytes 8388608 | tf_op jit(solution)/shard_map/smd,snd->smn/dot_general | solution.py:28
  144.8 5.5 gather_fusion.1
  150.3 0.1 copy.60
  150.4 6.1 broadcast_add_fusion
  156.5 5.2 copy.62
  161.8 5.2 copy.63
  167.0 5.6 add_multiply_fusion
  172.7 1.9 copy-done
  174.6 46.9 %custom-call.35 = f32[4,128,128]{2,1,0:T(8,128)S(1)} custom-call(f32[4,128,128]{2,1,0:T(8,128)S(1)} %cholesky.274), custom_call_target="Cholesky" | custom-call | tf_op jit(solution)/shard_map/jit(cholesky)/cholesky | solution.py:34
  221.5 39.8 %custom-call.36 = f32[4,1,128,128]{2,3,1,0:T(8,128)S(1)} custom-call(f32[4,1,128,128]{3,2,1,0:T(8,128)S(1)} %select_bitcast_fusion.2), custom_call_target="InvertDiagBlocksLowerTriangular" | custom-call | tf_op jit(solution)/shard_map/jit(cholesky)/cholesky | solution.py:34
  261.3 2.5 cholesky.234
  263.8 2.9 constant_dynamic-update-slice_fusion.6
  266.7 2.0 convolution_subtract_fusion
  268.7 46.9 %custom-call.37 = f32[4,128,128]{2,1,0:T(8,128)S(1)} custom-call(f32[4,128,128]{2,1,0:T(8,128)S(1)} %cholesky.278), custom_call_target="Cholesky" | custom-call | tf_op jit(solution)/shard_map/jit(cholesky)/cholesky | solution.py:34
  315.6 0.8 select_bitcast_fusion.1
  316.4 39.3 %custom-call.38 = f32[4,1,128,128]{2,3,1,0:T(8,128)S(1)} custom-call(f32[4,1,128,128]{3,2,1,0:T(8,128)S(1)} %get-tuple-element.32), custom_call_target="InvertDiagBlocksLowerTriangular" | custom-call | tf_op jit(solution)/shard_map/jit(cholesky)/cholesky | solution.py:34
  355.7 1.5 convolution_dynamic-update-slice_fusion
  357.2 2.6 convolution_subtract_fusion.2
  359.8 47.1 %custom-call.39 = f32[4,128,128]{2,1,0:T(8,128)S(1)} custom-call(f32[4,128,128]{2,1,0:T(8,128)S(1)} %cholesky.283), custom_call_target="Cholesky" | custom-call | tf_op jit(solution)/shard_map/jit(cholesky)/cholesky | solution.py:34
  406.9 0.8 select_bitcast_fusion
  407.7 39.3 %custom-call.40 = f32[4,1,128,128]{2,3,1,0:T(8,128)S(1)} custom-call(f32[4,1,128,128]{3,2,1,0:T(8,128)S(1)} %get-tuple-element.30), custom_call_target="InvertDiagBlocksLowerTriangular" | custom-call | tf_op jit(solution)/shard_map/jit(cholesky)/cholesky | solution.py:34
  447.0 1.1 convolution_dynamic-update-slice_fusion.1
  448.1 2.6 convolution_subtract_fusion.4
  450.7 47.1 %custom-call.41 = f32[4,128,128]{2,1,0:T(8,128)S(1)} custom-call(f32[4,128,128]{2,1,0:T(8,128)S(1)} %convolution_subtract_fusion.4), custom_call_target="Cholesky" | custom-call | tf_op jit(solution)/shard_map/jit(cholesky)/cholesky | solution.py:34
  497.8 0.9 select_reduce_fusion.2
  498.7 0.1 compare_reduce_fusion
  498.8 0.1 compare_reduce_fusion.1
  498.9 0.1 compare_reduce_fusion.2
  499.1 0.1 compare_reduce_fusion.3
  499.2 4.9 select_select_fusion
  504.1 15.0 %while.1 = (s32[]{:T(128)}, f32[4,512,512]{2,1,0:T(8,128)}, s32[4,2]{0,1:T(2,128)S(1)}, f32[4,4,128,128]{3,2,0,1:T(8,128)}, s32[]{:T(128)}) while((s32[]{:T(128)}, f32[4,512,512]{2,1,0:T(8,128)}, s32[4,2]{0,1:T(2,128)S(1)}, f32[4,4,128,128]{3,2,0,1:T(8,128)}, s32[]{:T(128)}) %tuple.30), condition=%wide.while_cond, body=%wide.while_body.sunk | while | flops 2 | bytes 525921 | solution.py:44
  504.2 0.5 fusion.52
  504.7 3.2 bitcast_dynamic-update-slice_fusion.2
  508.0 0.5 fusion.52
  508.5 3.2 bitcast_dynamic-update-slice_fusion.2
  511.7 0.5 fusion.52
  512.3 3.2 bitcast_dynamic-update-slice_fusion.2
  515.5 0.5 fusion.52
  516.0 3.1 bitcast_dynamic-update-slice_fusion.2
  519.1 158.0 %custom-call.42 = f32[4,4,128,128]{2,3,1,0:T(8,128)S(1)} custom-call(f32[4,4,128,128]{3,2,1,0:T(8,128)} %bitcast.74), custom_call_target="InvertDiagBlocksLowerTriangular" | custom-call | tf_op jit(solution)/shard_map/vmap(jit(_solve_triangular))/triangular_solve | solution.py:44
  677.1 0.6 fusion.27
  677.7 1.6 convolution_subtract_fusion.3
  679.3 0.6 fusion.29
  679.9 2.1 convolution_subtract_fusion.1
  682.0 0.6 fusion.30
  682.6 2.7 fusion.7
  685.3 0.6 fusion.31
  685.9 1.5 pad_maximum_fusion.1
  (32 shorter events, 0.6 us)
Async XLA Ops:
  0.0 17.6 %collective-permute-start = (bf16[32,32,256]{2,1,0:T(8,128)(2,1)}, bf16[32,32,256]{2,1,0:T(8,128)(2,1)S(1)}, u32[]{:S(2)}, u32[]{:S(2)}) collective-permute-start(bf16[32,32,256]{2,1,0:T(8,128)(2,1)} %param.4), channel_id=1, source_target_pairs={{0,8},{8,16},{16,24},{24,32},{32,40},{40,48},{48,56},{56,64},{64,7... | collective-permute-start | bytes 1572872 | tf_op jit(solution)/shard_map/ppermute | solution.py:19
  2.1 18.1 %collective-permute-start.1 = (bf16[32,32,256]{2,1,0:T(8,128)(2,1)}, bf16[32,32,256]{2,1,0:T(8,128)(2,1)S(1)}, u32[]{:S(2)}, u32[]{:S(2)}) collective-permute-start(bf16[32,32,256]{2,1,0:T(8,128)(2,1)} %param.4), channel_id=1, source_target_pairs={{8,0},{16,8},{24,16},{32,24},{40,32},{48,40},{56,48},{64,56},{72,6... | collective-permute-start | bytes 1572872 | tf_op jit(solution)/shard_map/ppermute | solution.py:22
  21.1 49.9 %collective-permute-start.2 = (bf16[96,32,256]{2,1,0:T(8,128)(2,1)}, bf16[96,32,256]{2,1,0:T(8,128)(2,1)}, u32[]{:S(2)}, u32[]{:S(2)}) collective-permute-start(bf16[96,32,256]{2,1,0:T(8,128)(2,1)} %constant_dynamic-update-slice_fusion), channel_id=1, source_target_pairs={{0,1},{1,2},{2,3},{3,4},{4,5},{5,6},{6,7},{7,0},{8,9},{9,10},{10,1... | collective-permute-start | bytes 4718600 | tf_op jit(solution)/shard_map/ppermute | solution.py:19
  23.9 47.1 %collective-permute-start.3 = (bf16[96,32,256]{2,1,0:T(8,128)(2,1)}, bf16[96,32,256]{2,1,0:T(8,128)(2,1)}, u32[]{:S(2)}, u32[]{:S(2)}) collective-permute-start(bf16[96,32,256]{2,1,0:T(8,128)(2,1)} %constant_dynamic-update-slice_fusion), channel_id=1, source_target_pairs={{1,0},{2,1},{3,2},{4,3},{5,4},{6,5},{7,6},{0,7},{9,8},{10,9},{11,1... | collective-permute-start | bytes 4718600 | tf_op jit(solution)/shard_map/ppermute | solution.py:22
  172.6 1.9 copy-start
where the time goes:
time: 699 us; the launch traced here: 688 us
  other arithmetic  491 us (70%)
  local copies, waits for them, and re-layouts  106 us (15%)
  blocking collectives  46.5 us (7%)
  matrix products  24.2 us (3%)
  waiting for transfers between devices  10.2 us (1%)
  starting transfers between devices  8.58 us (1%)
    another operation x18, other arithmetic, factor_blocks(): lower = jnp.linalg.cholesky(theta)  309 us
    another operation x5, other arithmetic, solve_one(): jax.scipy.linalg.solve_triangular(lower_one, target, lower=True, trans='T')  164 us
    dot_general x1, local copies, waits for them, and re-layouts, factor_blocks(): jnp.einsum('smd,snd->smn', point_set, point_set, preferred_element_type=j...  60.3 us
    all_gather x1, blocking collectives, body(): coarse = lax.all_gather(coarse_features, ('sx', 'sy'), axis=0, tiled=True)  46.5 us
    another operation x12, local copies, waits for them, and re-layouts  15 us
  transfers between devices with their start and end apart: 4, of which 1 were waited for; matrix products, arithmetic and copies ran while one was open for 1% of the time, Pallas kernels for 0%

commit v1 on v0

v1 whole, which is shorter than its diff:
```python
import jax
import jax.numpy as jnp
from jax import lax
from jax.experimental import pallas as pl
from jax.experimental.pallas import tpu as pltpu
from jax.sharding import PartitionSpec as P

SB = 16
REACH = 2
NUGGET = 0.3
BS = 32
F32 = jnp.float32
BF16 = jnp.bfloat16
HI = lax.Precision.HIGHEST
NN = (((1,), (0,)), ((), ()))
NT = (((1,), (1,)), ((), ()))


def mm(a, b, dims=NN):
    return lax.dot_general(a, b, dims, precision=HI, preferred_element_type=F32)


def bmm(a, b, dims=NN):
    return lax.dot_general(a, b, dims, preferred_element_type=F32)


def lane_pick(x, lane):
    at = (lax.broadcasted_iota(jnp.int32, x.shape, 1) // BS) * BS + lane
    return jnp.take_along_axis(x, at, axis=1)


def base_block(z):
    vs = [z[8 * v : 8 * v + 8] for v in range(4)]
    li = lax.broadcasted_iota(jnp.int32, (8, 128), 1) % BS
    si = lax.broadcasted_iota(jnp.int32, (8, 128), 0)
    factor = []
    for g in range(4):
        cols = [[lane_pick(vs[v], 8 * g + q) for v in range(4)] for q in range(8)]
        here = li // 8 == g
        eye = (li % 8 == si).astype(F32)
        vs = [jnp.where(here, eye if v == g else 0.0, vs[v]) for v in range(4)]
        rows = jnp.zeros((8, 128), F32)
        for q in range(8):
            piv = jnp.broadcast_to(cols[q][g][q : q + 1], (8, 128))
            rinv = 1.0 / piv
            plain = jnp.broadcast_to(vs[g][q : q + 1], (8, 128))
            rows = jnp.where(si == q, plain * lax.rsqrt(piv), rows)
            row = plain * rinv
            later = {p: jnp.broadcast_to(cols[p][g][q : q + 1], (8, 128)) * rinv for p in range(q + 1, 8)}
            for v in range(4):
                m = cols[q][v]
                vs[v] = vs[v] - m * row
                for p in later:
                    cols[p][v] = cols[p][v] - m * later[p]
                if v == g:
                    vs[v] = jnp.where(si == q, row, vs[v])
                    for p in later:
                        cols[p][v] = jnp.where(si == q, later[p], cols[p][v])
        factor.append(jnp.where(li <= si + 8 * g, rows, 0.0))
    return jnp.concatenate(vs, 0), jnp.concatenate(factor, 0)


def spread(x, diag):
    return jnp.where(diag, jnp.concatenate([x] * 4, 0), 0.0)


def inner(zp):
    diag = lax.broadcasted_iota(jnp.int32, (128, 128), 0) // BS == lax.broadcasted_iota(jnp.int32, (128, 128), 1) // BS
    zp = [[z[BS * t : BS * t + BS] for t in range(4)] for z in zp]
    out = []
    for t in range(4):
        dinv, w = base_block(zp[t][t])
        src = [spread(zp[u][t], diag) if u != t else None for u in range(4)]
        out.append([mm(w, src[u]) for u in range(t)] + [w] + [jnp.zeros_like(w)] * (3 - t))
        dspread = spread(dinv, diag)
        for i in range(t + 1, 4):
            g = mm(zp[t][i], dspread)
            for u in range(4):
                zp[u][i] = -g if u == t else zp[u][i] - mm(g, src[u])
    return out


def unpack(out, s):
    return jnp.concatenate(
        [jnp.concatenate([out[t][u][:, BS * s : BS * s + BS] for u in range(4)], 1) for t in range(4)], 0
    )


def pack(blocks):
    return [jnp.concatenate([b[:, BS * u : BS * u + BS] for b in blocks], 1) for u in range(4)]


def squares(x):
    xf = x.astype(F32)
    x2 = xf * xf
    hi = x2.astype(BF16)
    lo = (x2 - hi.astype(F32)).astype(BF16)
    ones = jnp.ones((8, x.shape[1]), BF16)
    row = (bmm(ones, hi, NT) + bmm(ones, lo, NT))[:1]
    return jnp.sum(x2, axis=1, keepdims=True), row


def theta(a, b, sa, sb, same):
    t = jnp.exp((2.0 * bmm(a, b, NT) - (sa + sb)) * (1.0 / a.shape[1]))
    if same:
        i, j = lax.broadcasted_iota(jnp.int32, t.shape, 0), lax.broadcasted_iota(jnp.int32, t.shape, 1)
        t = jnp.where(i == j, 1.0 + NUGGET, t)
    return t


def kernel(feat_ref, coarse_ref, fine_at_ref, own_at_ref, out_ref, acc_ref, fo_ref, k_ref, kt_ref, a_ref, lof_ref, e_ref):
    side = feat_ref.shape[0]
    width = feat_ref.shape[2]
    nf = 128
    pc = coarse_ref[...]
    sc_col, sc_row = squares(pc)
    acc_ref[...] = jnp.zeros_like(acc_ref)
    step_rows = 16
    chunk = step_rows * side

    def pick(c, carry):
        rows = feat_ref[pl.ds(c * step_rows, step_rows)].reshape(chunk, width)
        lane = lax.broadcasted_iota(jnp.int32, (4 * nf, chunk), 1) + c * chunk
        hot = jnp.where(lane == fine_at_ref[...], 1.0, 0.0).astype(BF16)
        acc_ref[...] += bmm(hot, rows)
        return carry

    lax.fori_loop(0, side // step_rows, pick, 0)
    for s in range(4):
        bx, by = divmod(s, 2)
        own = feat_ref[32 + 16 * bx : 48 + 16 * bx, 32 + 16 * by : 48 + 16 * by].reshape(256, width)
        hot = jnp.where(
            lax.broadcasted_iota(jnp.int32, (256, 256), 1) == own_at_ref[256 * s : 256 * s + 256], 1.0, 0.0
        ).astype(BF16)
        fo_ref[s, nf:] = bmm(hot, own).astype(BF16)
        fo_ref[s, :nf] = acc_ref[nf * s : nf * s + nf].astype(BF16)
    acc = theta(pc, pc, sc_col, sc_row, True)
    wc = unpack(inner(pack([acc] * 4)), 0)
    wct = wc.T
    for s in range(4):
        p = fo_ref[s]
        col, row = squares(p)
        kc = mm(theta(p, pc, col, sc_row, False), wc, NT)
        k_ref[s] = kc
        kt_ref[s] = mm(wc, theta(pc, p, sc_col, row, False))
        a_ref[s] = theta(p, p, col, row, True) - mm(kc, kc, NT)
    out = inner(pack([a_ref[s, :nf, :nf] for s in range(4)]))
    for s in range(4):
        wf = unpack(out, s)
        lof = mm(a_ref[s, nf:, :nf], wf, NT)
        lof_ref[s] = lof
        a_ref[s, nf:, nf:] = a_ref[s, nf:, nf:] - mm(lof, lof, NT)
        qft = mm(wf.T, mm(wf, a_ref[s, :nf, nf:]))
        e_ref[s, 128:256] = -qft
        e_ref[s, :128] = mm(wct, mm(kt_ref[s, :, :nf], qft) - kt_ref[s, :, nf:])
    out = inner(pack([a_ref[s, 128:256, 128:256] for s in range(4)]))
    for s in range(4):
        w0 = unpack(out, s)
        l10 = mm(a_ref[s, 256:, 128:256], w0, NT)
        lof_ref[s, :128] = l10
        a_ref[s, 256:, 256:] = a_ref[s, 256:, 256:] - mm(l10, l10, NT)
        top = mm(e_ref[s, :, :128], w0, NT)
        w0t = w0.T
        out_ref[s, :256, :128] = top
        out_ref[s, 256:384, :128] = w0t
        out_ref[s, 384:, :128] = jnp.zeros((128, 128), F32)
        e_ref[s, :, 128:] = e_ref[s, :, 128:] - mm(top, l10, NT)
        a_ref[s, :128, :128] = mm(w0t, l10, NT)
    out = inner(pack([a_ref[s, 256:, 256:] for s in range(4)]))
    for s in range(4):
        w1 = unpack(out, s)
        out_ref[s, :256, 128:] = mm(e_ref[s, :, 128:], w1, NT)
        out_ref[s, 256:384, 128:] = -mm(a_ref[s, :128, :128], w1, NT)
        out_ref[s, 384:, 128:] = w1.T


def padded_2(block, sides, width):
    for axis, dim in sides:
        count = lax.axis_size(axis)
        forward = [(i, (i + 1) % count) for i in range(count)]
        backward = [(target, source) for source, target in forward]
        low = lax.ppermute(
            lax.slice_in_dim(block, block.shape[dim] - width, None, axis=dim), axis, forward
        )
        high = lax.ppermute(lax.slice_in_dim(block, 0, width, axis=dim), axis, backward)
        block = jnp.concatenate([low, block, high], axis=dim)
    return block


def body(features, coarse_features, fine_index, own_order):
    block_x, block_y, fine_count = fine_index.shape
    rim = REACH * SB
    coarse = lax.all_gather(coarse_features, ("sx", "sy"), axis=0, tiled=True)
    padded = padded_2(features, (("sx", 0), ("sy", 1)), rim)
    side = padded.shape[1]
    win = (2 * REACH + 1) * SB
    start_x = (jnp.arange(block_x, dtype=jnp.int32) * SB)[:, None, None]
    start_y = (jnp.arange(block_y, dtype=jnp.int32) * SB)[None, :, None]
    fine_at = (start_x + fine_index // win) * side + start_y + fine_index % win
    vmem = pl.BlockSpec(memory_space=pltpu.VMEM)
    out = pl.pallas_call(
        kernel,
        out_shape=jax.ShapeDtypeStruct((4, 512, 256), F32),
        in_specs=[vmem] * 4,
        out_specs=vmem,
        scratch_shapes=[
            pltpu.VMEM((512, 256), F32),
            pltpu.VMEM((4, 384, 256), BF16),
            pltpu.VMEM((4, 384, 128), F32),
            pltpu.VMEM((4, 128, 384), F32),
            pltpu.VMEM((4, 384, 384), F32),
            pltpu.VMEM((4, 256, 128), F32),
            pltpu.VMEM((4, 256, 256), F32),
        ],
        compiler_params=pltpu.CompilerParams(vmem_limit_bytes=40 * 2**20),
    )(padded, coarse, fine_at.reshape(-1, 1), own_order.reshape(-1, 1))
    return out.reshape(block_x, block_y, 512, 256)


def solution(mesh):
    in_specs = (
        P("sx", "sy", None),
        P(("sx", "sy"), None),
        P("sx", "sy", None),
        P("sx", "sy", None),
    )
    out_specs = P("sx", "sy", None, None)
    return jax.shard_map(body, mesh=mesh, in_specs=in_specs, out_specs=out_specs, check_vma=False)
```

time: 699 us -> 110 us (0.16); the launches traced: 688 us -> 110 us
  other arithmetic: 491 us -> 2.15 us
  local copies, waits for them, and re-layouts: 106 us -> 1.67 us
  Pallas kernels: 0 us -> 40 us
  matrix products: 24.2 us -> 0 us
    another operation x23 -> x0, other arithmetic: 474 us -> none  [the longest x18 309 us: factor_blocks(): lower = jnp.linalg.cholesky(theta)]
    dot_general x1 -> x0, local copies, waits for them, and re-layouts: 60.3 us -> none  [factor_blocks(): jnp.einsum('smd,snd->smn', point_set, point_set, preferred_element_type=j...]
    pallas_call x0 -> x1, Pallas kernels: none -> 40 us  [body(): pl.pallas_call(kernel, out_shape=jax.ShapeDtypeStruct((4, 512, 256), F32)...]
    another operation x13 -> x0, matrix products: 21.5 us -> none  [the longest x6 12.7 us: factor_blocks(): lower = jnp.linalg.cholesky(theta)]
    another operation x18 -> x0, local copies, waits for them, and re-layouts: 17.6 us -> none
    gather x3 -> x0, local copies, waits for them, and re-layouts: 12.2 us -> none  [the longest x1 6.59 us: body(): gathered = jnp.take(flat_rows, chosen, axis=0)]
    add x3 -> x1, other arithmetic: 7.63 us -> 0.08 us  [body(): fine_at = (start_x + fine_index // win) * side + start_y + fine_index % win]
  transfers between devices with their start and end apart: 4 -> 4, of which waited for: 1 -> 1; matrix products, arithmetic and copies ran while one was open for 1% -> 2% of each run, Pallas kernels for 0% -> 0%
where the time goes in v1:
time: 110 us
  blocking collectives  45.7 us (42%)
  Pallas kernels  40 us (36%)
  waiting for transfers between devices  11.7 us (11%)
  starting transfers between devices  8.65 us (8%)
  other arithmetic  2.15 us (2%)
  local copies, waits for them, and re-layouts  1.67 us (2%)
    all_gather x1, blocking collectives, body(): coarse = lax.all_gather(coarse_features, ('sx', 'sy'), axis=0, tiled=True)  45.7 us
    pallas_call x1, Pallas kernels, body(): pl.pallas_call(kernel, out_shape=jax.ShapeDtypeStruct((4, 512, 256), F32)...  40 us
    ppermute x2, waiting for transfers between devices, padded_2(): lax.ppermute(lax.slice_in_dim(block, block.shape[dim] - width, None, axis...  11.7 us
    ppermute x2, starting transfers between devices, padded_2(): lax.ppermute(lax.slice_in_dim(block, block.shape[dim] - width, None, axis...  4.95 us
    ppermute x2, starting transfers between devices, padded_2(): lax.ppermute(lax.slice_in_dim(block, 0, width, axis=dim), axis, backward)  3.7 us
  transfers between devices with their start and end apart: 4, of which 1 were waited for; matrix products, arithmetic and copies ran while one was open for 2% of the time, Pallas kernels for 0%

profile of v1, /device:TPU:1, one launch (start us, length us, event | category | flops | bytes accessed | tf_op | source)
XLA Modules:
  0.0 110.0 jit_solution(16228020947721926646)
XLA Ops:
  0.0 0.0 copy-start
  0.0 2.1 %collective-permute-start = (bf16[32,32,256]{2,1,0:T(8,128)(2,1)}, bf16[32,32,256]{2,1,0:T(8,128)(2,1)S(1)}, u32[]{:S(2)}, u32[]{:S(2)}) collective-permute-start(bf16[32,32,256]{2,1,0:T(8,128)(2,1)} %param.4), channel_id=1, source_target_pairs={{0,8},{8,16},{16,24},{24,32},{32,40},{40,48},{48,56},{56,64},{64,7... | collective-permute-start | bytes 1572872 | tf_op jit(solution)/shard_map/ppermute | solution.py:182
  2.1 3.7 %collective-permute-start.1 = (bf16[32,32,256]{2,1,0:T(8,128)(2,1)}, bf16[32,32,256]{2,1,0:T(8,128)(2,1)S(1)}, u32[]{:S(2)}, u32[]{:S(2)}) collective-permute-start(bf16[32,32,256]{2,1,0:T(8,128)(2,1)} %param.4), channel_id=1, source_target_pairs={{8,0},{16,8},{24,16},{32,24},{40,32},{48,40},{56,48},{64,56},{72,6... | collective-permute-start | bytes 1572872 | tf_op jit(solution)/shard_map/ppermute | solution.py:185
  5.8 11.7 %collective-permute-done = bf16[32,32,256]{2,1,0:T(8,128)(2,1)S(1)} collective-permute-done((bf16[32,32,256]{2,1,0:T(8,128)(2,1)}, bf16[32,32,256]{2,1,0:T(8,128)(2,1)S(1)}, u32[]{:S(2)}, u32[]{:S(2)}) %collective-permute-start) | collective-permute-done | bytes 524320 | tf_op jit(solution)/shard_map/ppermute | solution.py:182
  17.6 0.0 copy-start.1
  17.6 0.0 copy-start.2
  17.6 1.1 constant_dynamic-update-slice_fusion.1
  18.7 0.0 collective-permute-done.1
  18.8 2.8 %collective-permute-start.2 = (bf16[96,32,256]{2,1,0:T(8,128)(2,1)S(1)}, bf16[96,32,256]{2,1,0:T(8,128)(2,1)}, u32[]{:S(2)}, u32[]{:S(2)}) collective-permute-start(bf16[96,32,256]{2,1,0:T(8,128)(2,1)S(1)} %constant_dynamic-update-slice_fusion), channel_id=1, source_target_pairs={{0,1},{1,2},{2,3},{3,4},{4,5},{5,6},{6,7},{7,0},{8,9},{9,10},{10,1... | collective-permute-start | bytes 4718600 | tf_op jit(solution)/shard_map/ppermute | solution.py:182
  21.6 0.0 collective-permute-start.3
  21.6 0.0 copy-done
  21.6 0.3 reshape.22.own_at_ref
  22.0 0.0 copy-done.1
  22.0 0.1 fusion
  22.0 0.1 copy.9.fine_at_ref
  22.2 0.0 copy-done.2
  22.2 45.7 %all-gather = bf16[128,1,256]{2,1,0:T(2,128)(2,1)S(1)} all-gather(bf16[1,1,256]{2,1,0:T(2,128)(2,1)S(1)} %bitcast.8), channel_id=1, replica_groups=mesh['sx'=16,'sy'=8] {'sx','sy'}, dimensions={0}, use_global_device_ids=true | all-gather | bytes 66048 | tf_op jit(solution)/shard_map/all_gather | solution.py:193
  68.0 0.0 collective-permute-done.2
  68.0 0.0 collective-permute-done.3
  68.0 2.1 %pad_maximum_fusion.feat_ref = bf16[96,96,256]{2,1,0:T(8,128)(2,1)S(1)} fusion(bf16[96,32,256]{2,1,0:T(8,128)(2,1)} %collective-permute-done.3, bf16[96,32,256]{2,1,0:T(8,128)(2,1)S(1)} %constant_dynamic-update-slice_fusion, bf16[96,32,256]{2,1,0:T(8,128)(2,1)} %collective-permute-done.2), kind=kLoop, calls=%fused_computation | loop fusion | flops 14155776 | bytes 9437184 | tf_op jit(solution)/shard_map/concatenate | solution.py:186
  70.1 40.0 %shard_map.46 = f32[4,512,256]{2,1,0:T(8,128)} custom-call(bf16[96,96,256]{2,1,0:T(8,128)(2,1)S(1)} %pad_maximum_fusion.feat_ref, bf16[128,256]{1,0:T(8,128)(2,1)S(1)} %bitcast.6, s32[512,1]{1,0:T(8,128)S(1)} %copy.9.fine_at_ref, s32[1024,1]{1,0:T(8,128)S(1)} %reshape.22.own_at_ref), custom_call_target="tpu_custom_call" | custom-call | tf_op jit(solution)/shard_map/pallas_call | solution.py:201
  (4 shorter events, 0.1 us)
Async XLA Ops:
  0.0 21.6 %copy-start = (s32[2,2,256]{2,1,0:T(2,128)S(1)}, s32[2,2,256]{2,1,0:T(2,128)}, u32[]{:S(2)}) copy-start(s32[2,2,256]{2,1,0:T(2,128)} %param.7) | copy-start | bytes 12292
  0.0 17.6 %collective-permute-start = (bf16[32,32,256]{2,1,0:T(8,128)(2,1)}, bf16[32,32,256]{2,1,0:T(8,128)(2,1)S(1)}, u32[]{:S(2)}, u32[]{:S(2)}) collective-permute-start(bf16[32,32,256]{2,1,0:T(8,128)(2,1)} %param.4), channel_id=1, source_target_pairs={{0,8},{8,16},{16,24},{24,32},{32,40},{40,48},{48,56},{56,64},{64,7... | collective-permute-start | bytes 1572872 | tf_op jit(solution)/shard_map/ppermute | solution.py:182
  2.1 16.6 %collective-permute-start.1 = (bf16[32,32,256]{2,1,0:T(8,128)(2,1)}, bf16[32,32,256]{2,1,0:T(8,128)(2,1)S(1)}, u32[]{:S(2)}, u32[]{:S(2)}) collective-permute-start(bf16[32,32,256]{2,1,0:T(8,128)(2,1)} %param.4), channel_id=1, source_target_pairs={{8,0},{16,8},{24,16},{32,24},{40,32},{48,40},{56,48},{64,56},{72,6... | collective-permute-start | bytes 1572872 | tf_op jit(solution)/shard_map/ppermute | solution.py:185
  17.6 4.4 %copy-start.1 = (s32[2,2,128]{2,1,0:T(2,128)S(1)}, s32[2,2,128]{2,1,0:T(2,128)}, u32[]{:S(2)}) copy-start(s32[2,2,128]{2,1,0:T(2,128)} %param.6) | copy-start | bytes 6148
  17.6 4.6 %copy-start.2 = (bf16[1,256]{1,0:T(2,128)(2,1)S(1)}, bf16[1,256]{1,0:T(2,128)(2,1)}, u32[]{:S(2)}) copy-start(bf16[1,256]{1,0:T(2,128)(2,1)} %param.5) | copy-start | bytes 1540
  18.8 49.2 %collective-permute-start.2 = (bf16[96,32,256]{2,1,0:T(8,128)(2,1)S(1)}, bf16[96,32,256]{2,1,0:T(8,128)(2,1)}, u32[]{:S(2)}, u32[]{:S(2)}) collective-permute-start(bf16[96,32,256]{2,1,0:T(8,128)(2,1)S(1)} %constant_dynamic-update-slice_fusion), channel_id=1, source_target_pairs={{0,1},{1,2},{2,3},{3,4},{4,5},{5,6},{6,7},{7,0},{8,9},{9,10},{10,1... | collective-permute-start | bytes 4718600 | tf_op jit(solution)/shard_map/ppermute | solution.py:182
  21.6 46.4 %collective-permute-start.3 = (bf16[96,32,256]{2,1,0:T(8,128)(2,1)S(1)}, bf16[96,32,256]{2,1,0:T(8,128)(2,1)}, u32[]{:S(2)}, u32[]{:S(2)}) collective-permute-start(bf16[96,32,256]{2,1,0:T(8,128)(2,1)S(1)} %constant_dynamic-update-slice_fusion), channel_id=1, source_target_pairs={{1,0},{2,1},{3,2},{4,3},{5,4},{6,5},{7,6},{0,7},{9,8},{10,9},{11,1... | collective-permute-start | bytes 4718600 | tf_op jit(solution)/shard_map/ppermute | solution.py:185

commit v2 on v1

--- a/solution.py
+++ b/solution.py
@@ -14,6 +14,8 @@
 HI = lax.Precision.HIGHEST
 NN = (((1,), (0,)), ((), ()))
 NT = (((1,), (1,)), ((), ()))
+MESH = pl.DeviceIdType.MESH
+CHUNKS = 4
 
 
 def mm(a, b, dims=NN):
@@ -112,7 +114,7 @@
     side = feat_ref.shape[0]
     width = feat_ref.shape[2]
     nf = 128
-    pc = coarse_ref[...]
+    pc = coarse_ref[...].reshape(128, width).astype(BF16)
     sc_col, sc_row = squares(pc)
     acc_ref[...] = jnp.zeros_like(acc_ref)
     step_rows = 16
@@ -174,24 +176,101 @@
         out_ref[s, 384:, 128:] = w1.T
 
 
-def padded_2(block, sides, width):
-    for axis, dim in sides:
-        count = lax.axis_size(axis)
-        forward = [(i, (i + 1) % count) for i in range(count)]
-        backward = [(target, source) for source, target in forward]
-        low = lax.ppermute(
-            lax.slice_in_dim(block, block.shape[dim] - width, None, axis=dim), axis, forward
+def comm_kernel(feat_ref, coarse_ref, win_ref, all_ref, row_ref, a_send, a_recv, b_send, b_recv, x_send, x_recv, y_send, y_recv, f_send, f_recv, own_sem):
+    nx, ny = lax.axis_size("sx"), lax.axis_size("sy")
+    i, j = lax.axis_index("sx"), lax.axis_index("sy")
+    rows, cols = feat_ref.shape[:2]
+    part = rows // CHUNKS
+
+    def at_x(step):
+        return {"sx": lax.rem(i + step + nx, nx), "sy": j}
+
+    def at_y(step):
+        return {"sx": i, "sy": lax.rem(j + step + ny, ny)}
+
+    def send(src, dst, s_sem, r_sem, device):
+        copy = pltpu.make_async_remote_copy(
+            src_ref=src, dst_ref=dst, send_sem=s_sem, recv_sem=r_sem, device_id=device, device_id_type=MESH
         )
-        high = lax.ppermute(lax.slice_in_dim(block, 0, width, axis=dim), axis, backward)
-        block = jnp.concatenate([low, block, high], axis=dim)
-    return block
+        copy.start()
+        return copy
+
+    barrier = pltpu.get_barrier_semaphore()
+    for k in range(1, ny):
+        pl.semaphore_signal(barrier, inc=1, device_id=at_y(k), device_id_type=MESH)
+    for k in range(1, nx):
+        pl.semaphore_signal(barrier, inc=1, device_id=at_x(k), device_id_type=MESH)
+    mine = pltpu.make_async_copy(feat_ref, win_ref.at[pl.ds(rows, rows), pl.ds(cols, cols)], own_sem.at[0])
+    mine.start()
+    row_ref[0] = coarse_ref[...].astype(F32)
+    pl.semaphore_wait(barrier, nx + ny - 2)
+    stage_a = [
+        send(row_ref, all_ref.at[i, pl.ds(j, 1)], a_send.at[k], a_recv.at[k], at_y(k)) for k in range(1, ny)
+    ]
+    keep = pltpu.make_async_copy(row_ref, all_ref.at[i, pl.ds(j, 1)], own_sem.at[1])
+    keep.start()
+    along_x = []
+    for c in range(CHUNKS):
+        for d, step in enumerate((1, -1)):
+            src = feat_ref.at[pl.ds(c * part, part)]
+            dst = win_ref.at[pl.ds(2 * rows * d + c * part, part), pl.ds(cols, cols)]
+            along_x.append(send(src, dst, x_send.at[d, c], x_recv.at[d, c], at_x(step)))
+    along_y = []
+    for d, step in enumerate((1, -1)):
+        dst = win_ref.at[pl.ds(rows, rows), pl.ds(2 * cols * d, cols)]
+        along_y.append(send(feat_ref, dst, y_send.at[d], y_recv.at[d], at_y(step)))
+    keep.wait()
+    for copy in stage_a:
+        copy.wait()
+    stage_b = [send(all_ref.at[i], all_ref.at[i], b_send.at[k], b_recv.at[k], at_x(k)) for k in range(1, nx)]
+    onward = []
+    for c in range(CHUNKS):
+        for e in range(2):
+            along_x[2 * c + e].wait()
+            src = win_ref.at[pl.ds(2 * rows * e + c * part, part), pl.ds(cols, cols)]
+            for d, step in enumerate((1, -1)):
+                dst = win_ref.at[pl.ds(2 * rows * e + c * part, part), pl.ds(2 * cols * d, cols)]
+                onward.append(send(src, dst, f_send.at[e, d, c], f_recv.at[e, d, c], at_y(step)))
+    mine.wait()
+    for copy in stage_b + along_y + onward:
+        copy.wait()
+
+
+def exchange(features, coarse_features):
+    nx, ny = lax.axis_size("sx"), lax.axis_size("sy")
+    rows, cols, width = features.shape
+    dma = pltpu.SemaphoreType.DMA
+    hbm = pl.BlockSpec(memory_space=pl.ANY)
+    return pl.pallas_call(
+        comm_kernel,
+        out_shape=(
+            jax.ShapeDtypeStruct((3 * rows, 3 * cols, width), features.dtype),
+            jax.ShapeDtypeStruct((nx, ny, 1, width), F32),
+        ),
+        in_specs=[hbm, pl.BlockSpec(memory_space=pltpu.VMEM)],
+        out_specs=(hbm, hbm),
+        scratch_shapes=[
+            pltpu.VMEM((1, 1, width), F32),
+            dma((ny,)),
+            dma((ny,)),
+            dma((nx,)),
+            dma((nx,)),
+            dma((2, CHUNKS)),
+            dma((2, CHUNKS)),
+            dma((2,)),
+            dma((2,)),
+            dma((2, 2, CHUNKS)),
+            dma((2, 2, CHUNKS)),
+            dma((2,)),
+        ],
+        compiler_params=pltpu.CompilerParams(collective_id=0, has_side_effects=True),
+    )(features, coarse_features)
 
 
 def body(features, coarse_features, fine_index, own_order):
     block_x, block_y, fine_count = fine_index.shape
-    rim = REACH * SB
-    coarse = lax.all_gather(coarse_features, ("sx", "sy"), axis=0, tiled=True)
-    padded = padded_2(features, (("sx", 0), ("sy", 1)), rim)
+    padded, coarse = exchange(features, coarse_features)
+    coarse = coarse.reshape(-1, 1, coarse.shape[3])
     side = padded.shape[1]
     win = (2 * REACH + 1) * SB
     start_x = (jnp.arange(block_x, dtype=jnp.int32) * SB)[:, None, None]

time: 110 us -> 77 us (0.70)
  blocking collectives: 45.7 us -> 0 us
  Pallas kernels: 40 us -> 71.6 us
  waiting for transfers between devices: 11.7 us -> 0 us
  starting transfers between devices: 8.65 us -> 0 us
  local copies, waits for them, and re-layouts: 1.67 us -> 4.42 us
  other arithmetic: 2.15 us -> 0.76 us
    all_gather x1 -> x0, blocking collectives: 45.7 us -> none  [body(): coarse = lax.all_gather(coarse_features, ('sx', 'sy'), axis=0, tiled=True)]
    pallas_call x0 -> x1, Pallas kernels: none -> 31.1 us  [exchange(): pl.pallas_call(comm_kernel, out_shape=(jax.ShapeDtypeStruct((3 * rows, 3...]
    ppermute x4 -> x0, waiting for transfers between devices: 11.7 us -> none  [the longest x2 11.7 us: padded_2(): lax.ppermute(lax.slice_in_dim(block, block.shape[dim] - width, None, axis...]
    ppermute x4 -> x0, starting transfers between devices: 8.65 us -> none  [the longest x2 4.95 us: padded_2(): lax.ppermute(lax.slice_in_dim(block, block.shape[dim] - width, None, axis...]
    unnamed x9 -> x4, local copies, waits for them, and re-layouts: 1.15 us -> 3.23 us
    concatenate x1 -> x0, other arithmetic: 2.07 us -> none  [padded_2(): block = jnp.concatenate([low, block, high], axis=dim)]
  transfers between devices with their start and end apart: 4 -> 0, of which waited for: 1 -> 0; matrix products, arithmetic and copies ran while one was open for 2% -> 0% of each run, Pallas kernels for 0% -> 0%
where the time goes in v2:
time: 77 us; the launch traced here: 76.8 us
  Pallas kernels  71.6 us (93%)
  local copies, waits for them, and re-layouts  4.42 us (6%)
    pallas_call x1, Pallas kernels, body(): pl.pallas_call(kernel, out_shape=jax.ShapeDtypeStruct((4, 512, 256), F32)...  40.4 us
    pallas_call x1, Pallas kernels, exchange(): pl.pallas_call(comm_kernel, out_shape=(jax.ShapeDtypeStruct((3 * rows, 3...  31.1 us
    unnamed x4, local copies, waits for them, and re-layouts  3.23 us

profile of v2, /device:TPU:1, one launch (start us, length us, event | category | flops | bytes accessed | tf_op | source)
XLA Modules:
  0.0 76.8 jit_solution(893240036031630605)
XLA Ops:
  0.0 0.8 fusion
  0.8 0.1 copy.5.fine_at_ref
  0.9 1.0 %reshape.24.own_at_ref = s32[1024,1]{1,0:T(8,128)S(1)} reshape(s32[2,2,256]{2,1,0:T(2,128)} %param.7) | data formatting | bytes 8192 | tf_op jit(solution)/shard_map/reshape | solution.py:295
  2.0 31.1 %shard_map.46 = (bf16[96,96,256]{2,1,0:T(8,128)(2,1)}, f32[16,8,1,256]{3,2,1,0:T(1,128)}) custom-call(bf16[32,32,256]{2,1,0:T(8,128)(2,1)} %feat_ref.1, bf16[1,256]{1,0:T(2,128)(2,1)} %coarse_ref.1), custom_call_target="tpu_custom_call" | custom-call | tf_op jit(solution)/shard_map/pallas_call | solution.py:244
  33.1 0.0 copy-start
  33.1 2.3 %copy-done = bf16[96,96,256]{2,1,0:T(8,128)(2,1)S(1)} copy-done((bf16[96,96,256]{2,1,0:T(8,128)(2,1)S(1)}, bf16[96,96,256]{2,1,0:T(8,128)(2,1)}, u32[]{:S(2)}) %copy-start) | copy-done | bytes 4718616
  35.5 0.0 copy-start.1
  35.5 0.9 %copy-done.1 = f32[16,8,1,256]{3,2,1,0:T(1,128)S(1)} copy-done((f32[16,8,1,256]{3,2,1,0:T(1,128)S(1)}, f32[16,8,1,256]{3,2,1,0:T(1,128)}, u32[]{:S(2)}) %copy-start.1) | copy-done | bytes 131096
  36.4 40.4 %shard_map.47 = f32[4,512,256]{2,1,0:T(8,128)} custom-call(bf16[96,96,256]{2,1,0:T(8,128)(2,1)S(1)} %copy-done, f32[128,1,256]{2,1,0:T(1,128)S(1)} %bitcast.3, s32[512,1]{1,0:T(8,128)S(1)} %copy.5.fine_at_ref, s32[1024,1]{1,0:T(8,128)S(1)} %reshape.24.own_at_ref), custom_call_target="tpu_custom_call" | custom-call | tf_op jit(solution)/shard_map/pallas_call | solution.py:280
  (1 shorter events, 0.0 us)
Async XLA Ops:
  33.1 2.3 %copy-start = (bf16[96,96,256]{2,1,0:T(8,128)(2,1)S(1)}, bf16[96,96,256]{2,1,0:T(8,128)(2,1)}, u32[]{:S(2)}) copy-start(bf16[96,96,256]{2,1,0:T(8,128)(2,1)} %get-tuple-element.7.feat_ref) | copy-start | bytes 14155780
  35.5 0.9 %copy-start.1 = (f32[16,8,1,256]{3,2,1,0:T(1,128)S(1)}, f32[16,8,1,256]{3,2,1,0:T(1,128)}, u32[]{:S(2)}) copy-start(f32[16,8,1,256]{3,2,1,0:T(1,128)} %get-tuple-element.8) | copy-start | bytes 393220

commit v3 on v1

--- a/solution.py
+++ b/solution.py
@@ -14,6 +14,7 @@
 HI = lax.Precision.HIGHEST
 NN = (((1,), (0,)), ((), ()))
 NT = (((1,), (1,)), ((), ()))
+MESH = pl.DeviceIdType.MESH
 
 
 def mm(a, b, dims=NN):
@@ -108,32 +109,25 @@
     return t
 
 
-def kernel(feat_ref, coarse_ref, fine_at_ref, own_at_ref, out_ref, acc_ref, fo_ref, k_ref, kt_ref, a_ref, lof_ref, e_ref):
-    side = feat_ref.shape[0]
+def column(x):
+    x = x.astype(F32)
+    pad = jnp.zeros((8 - x.shape[0], x.shape[1]), F32)
+    return jnp.concatenate([x, pad], 0).T
+
+
+def kernel(feat_ref, coarse_ref, fine_ref, own_at_ref, out_ref, fo_ref, k_ref, kt_ref, a_ref, lof_ref, e_ref):
     width = feat_ref.shape[2]
     nf = 128
     pc = coarse_ref[...]
     sc_col, sc_row = squares(pc)
-    acc_ref[...] = jnp.zeros_like(acc_ref)
-    step_rows = 16
-    chunk = step_rows * side
-
-    def pick(c, carry):
-        rows = feat_ref[pl.ds(c * step_rows, step_rows)].reshape(chunk, width)
-        lane = lax.broadcasted_iota(jnp.int32, (4 * nf, chunk), 1) + c * chunk
-        hot = jnp.where(lane == fine_at_ref[...], 1.0, 0.0).astype(BF16)
-        acc_ref[...] += bmm(hot, rows)
-        return carry
-
-    lax.fori_loop(0, side // step_rows, pick, 0)
+    own_at = column(own_at_ref[...])
+    lane = lax.broadcasted_iota(jnp.int32, (256, 256), 1).astype(F32)
     for s in range(4):
         bx, by = divmod(s, 2)
-        own = feat_ref[32 + 16 * bx : 48 + 16 * bx, 32 + 16 * by : 48 + 16 * by].reshape(256, width)
-        hot = jnp.where(
-            lax.broadcasted_iota(jnp.int32, (256, 256), 1) == own_at_ref[256 * s : 256 * s + 256], 1.0, 0.0
-        ).astype(BF16)
+        own = feat_ref[SB * bx : SB * bx + SB, SB * by : SB * by + SB].reshape(256, width)
+        hot = jnp.where(lane == own_at[:, s : s + 1], 1.0, 0.0).astype(BF16)
         fo_ref[s, nf:] = bmm(hot, own).astype(BF16)
-        fo_ref[s, :nf] = acc_ref[nf * s : nf * s + nf].astype(BF16)
+        fo_ref[s, :nf] = fine_ref[nf * s : nf * s + nf]
     acc = theta(pc, pc, sc_col, sc_row, True)
     wc = unpack(inner(pack([acc] * 4)), 0)
     wct = wc.T
@@ -174,6 +168,166 @@
         out_ref[s, 384:, 128:] = w1.T
 
 
+OFFS = ((-1, -1), (-1, 0), (-1, 1), (0, -1), (0, 1), (1, -1), (1, 0), (1, 1))
+CAPS = tuple(112 if 0 in o else 96 for o in OFFS)
+STARTS = tuple(sum(CAPS[:n]) for n in range(9))
+
+
+def comm_kernel(
+    feat_ref, coarse_ref, fine_at_ref, fine_ref, coarse_out_ref, flag_ref,
+    tile_ref, row_ref, all_ref, code_ref, codes_ref, out_ref, in_ref,
+    a_send, a_recv, b_send, b_recv, c_send, c_recv, d_send, d_recv, tile_sem,
+):
+    nx, ny = lax.axis_size("sx"), lax.axis_size("sy")
+    i, j = lax.axis_index("sx"), lax.axis_index("sy")
+    rows, cols, width = feat_ref.shape
+    cells = rows * cols
+    asked = fine_at_ref.shape[0] * fine_at_ref.shape[1]
+
+    def at(dx, dy):
+        return {"sx": lax.rem(i + dx + nx, nx), "sy": lax.rem(j + dy + ny, ny)}
+
+    def send(src, dst, s_sem, r_sem, device):
+        copy = pltpu.make_async_remote_copy(
+            src_ref=src, dst_ref=dst, send_sem=s_sem, recv_sem=r_sem, device_id=device, device_id_type=MESH
+        )
+        copy.start()
+        return copy
+
+    load = pltpu.make_async_copy(feat_ref, tile_ref, tile_sem)
+    load.start()
+    barrier = pltpu.get_barrier_semaphore()
+    partners = [(dx, dy) for dx, dy in OFFS if dx and dy]
+    partners += [(0, k) for k in range(1, ny)] + [(k, 0) for k in range(1, nx)]
+    for dx, dy in partners:
+        pl.semaphore_signal(barrier, inc=1, device_id=at(dx, dy), device_id_type=MESH)
+
+    f = fine_at_ref[...]
+    win_row = lax.shift_right_logical(f * 52429, 22)
+    s_at = lax.broadcasted_iota(jnp.int32, f.shape, 0)
+    r = win_row + SB * lax.shift_right_logical(s_at, 1)
+    c = f - 80 * win_row + SB * lax.bitwise_and(s_at, 1)
+    t9 = 3 * lax.shift_right_logical(r, 5) + lax.shift_right_logical(c, 5)
+    code = cells * t9 + 32 * lax.bitwise_and(r, 31) + lax.bitwise_and(c, 31)
+    code = code.astype(F32)
+    code = jnp.concatenate([code[s : s + 1] for s in range(4)], 1)
+    code_ref[0] = code
+    before = jnp.where(
+        lax.broadcasted_iota(jnp.int32, (asked, asked), 0) < lax.broadcasted_iota(jnp.int32, (asked, asked), 1), 1.0, 0.0
+    ).astype(BF16)
+    slot_at = lax.broadcasted_iota(jnp.int32, (8, asked), 0)
+
+    def by_slot(values):
+        out = jnp.zeros((8, asked), F32)
+        for n, value in enumerate(values):
+            out = jnp.where(slot_at == n, float(value), out)
+        return out
+
+    def ranks(offset):
+        ok = jnp.logical_and(offset >= 0.0, offset < cells)
+        return ok, bmm(jnp.where(ok, 1.0, 0.0).astype(BF16), before)
+
+    offset = jnp.broadcast_to(code, (8, asked)) - by_slot([cells * (3 * (dx + 1) + dy + 1) for dx, dy in OFFS])
+    ok, rank = ranks(offset)
+    late = jnp.where(jnp.logical_and(ok, rank >= by_slot(CAPS)), 1.0, 0.0)
+    late = jnp.sum(jnp.sum(late, axis=1, keepdims=True), axis=0, keepdims=True)
+    slot = jnp.sum(jnp.where(ok, rank + by_slot(STARTS[:8]), 0.0), axis=0, keepdims=True)
+    local = code - 4.0 * cells
+    inside = jnp.logical_and(local >= 0.0, local < cells)
+    where_at = column(jnp.concatenate([jnp.where(inside, -1.0, slot), jnp.where(inside, local, -1.0)], 0))
+    row_ref[0, :, :width] = coarse_ref[...].astype(F32)
+    row_ref[0, :, width:] = jnp.broadcast_to(late, (1, 128))
+    pl.semaphore_wait(barrier, len(partners))
+
+    asks = [
+        send(code_ref, codes_ref.at[pl.ds(7 - n, 1)], c_send.at[n], c_recv.at[7 - n], at(*OFFS[n])) for n in range(8)
+    ]
+    stage_a = [
+        send(row_ref, all_ref.at[i, pl.ds(j, 1)], a_send.at[k], a_recv.at[k], at(0, k)) for k in range(1, ny)
+    ]
+    all_ref[i, pl.ds(j, 1)] = row_ref[...]
+    load.wait()
+    tile = tile_ref[...].reshape(cells, width)
+    lane = lax.broadcasted_iota(jnp.int32, (asked, cells), 1).astype(F32)
+    fine = bmm(jnp.where(lane == where_at[:, 1:2], 1.0, 0.0).astype(BF16), tile)
+    for ask in asks:
+        ask.wait()
+    codes = jnp.concatenate([codes_ref[n] for n in range(8)], 0)
+    offset = codes - by_slot([cells * (3 * (1 - dx) + 1 - dy) for dx, dy in OFFS])
+    ok, rank = ranks(offset)
+    rank = jnp.where(ok, rank, -1.0)
+    for copy in stage_a:
+        copy.wait()
+    stage_b = [send(all_ref.at[i], all_ref.at[i], b_send.at[k], b_recv.at[k], at(k, 0)) for k in range(1, nx)]
+    moves = []
+    for n in (0, 2, 5, 7, 1, 6, 3, 4):
+        cap = CAPS[n]
+        slots = lax.broadcasted_iota(jnp.int32, (cap, asked), 0).astype(F32)
+        cell = jnp.sum(jnp.where(slots == rank[n : n + 1], offset[n : n + 1], 0.0), axis=1, keepdims=True)
+        hot = jnp.where(lane[:cap] == cell, 1.0, 0.0).astype(BF16)
+        out_ref[STARTS[n] : STARTS[n + 1]] = bmm(hot, tile).astype(BF16)
+        moves.append(
+            send(
+                out_ref.at[pl.ds(STARTS[n], cap)],
+                in_ref.at[pl.ds(STARTS[7 - n], cap)],
+                d_send.at[n],
+                d_recv.at[7 - n],
+                at(*OFFS[n]),
+            )
+        )
+    for copy in stage_b:
+        copy.wait()
+    full = all_ref[...].reshape(nx * ny, width + 128)
+    coarse_out_ref[...] = full[:, :width].astype(BF16)
+    flag_ref[...] = jnp.sum(full[:, width:], axis=0, keepdims=True)
+    for copy in moves:
+        copy.wait()
+    got = in_ref[...]
+    lane = lax.broadcasted_iota(jnp.int32, (asked, got.shape[0]), 1).astype(F32)
+    fine = fine + bmm(jnp.where(lane == where_at[:, :1], 1.0, 0.0).astype(BF16), got)
+    fine_ref[...] = fine.astype(BF16)
+
+
+def exchange(features, coarse_features, fine_at):
+    nx, ny = lax.axis_size("sx"), lax.axis_size("sy")
+    rows, cols, width = features.shape
+    asked = fine_at.shape[0] * fine_at.shape[1]
+    dma = pltpu.SemaphoreType.DMA
+    hbm = pl.BlockSpec(memory_space=pl.ANY)
+    vmem = pl.BlockSpec(memory_space=pltpu.VMEM)
+    return pl.pallas_call(
+        comm_kernel,
+        out_shape=(
+            jax.ShapeDtypeStruct((asked, width), BF16),
+            jax.ShapeDtypeStruct((nx * ny, width), BF16),
+            jax.ShapeDtypeStruct((1, 128), F32),
+        ),
+        in_specs=[hbm, vmem, vmem],
+        out_specs=(vmem, vmem, vmem),
+        scratch_shapes=[
+            pltpu.VMEM((rows, cols, width), BF16),
+            pltpu.VMEM((1, 1, width + 128), F32),
+            pltpu.VMEM((nx, ny, 1, width + 128), F32),
+            pltpu.VMEM((1, 1, asked), F32),
+            pltpu.VMEM((8, 1, asked), F32),
+            pltpu.VMEM((STARTS[8], width), BF16),
+            pltpu.VMEM((STARTS[8], width), BF16),
+            dma((ny,)),
+            dma((ny,)),
+            dma((nx,)),
+            dma((nx,)),
+            dma((8,)),
+            dma((8,)),
+            dma((8,)),
+            dma((8,)),
+            dma,
+        ],
+        compiler_params=pltpu.CompilerParams(
+            collective_id=0, has_side_effects=True, vmem_limit_bytes=32 * 2**20
+        ),
+    )(features, coarse_features, fine_at)
+
+
 def padded_2(block, sides, width):
     for axis, dim in sides:
         count = lax.axis_size(axis)
@@ -187,16 +341,21 @@
     return block
 
 
-def body(features, coarse_features, fine_index, own_order):
-    block_x, block_y, fine_count = fine_index.shape
-    rim = REACH * SB
-    coarse = lax.all_gather(coarse_features, ("sx", "sy"), axis=0, tiled=True)
-    padded = padded_2(features, (("sx", 0), ("sy", 1)), rim)
-    side = padded.shape[1]
+def whole_tiles(features, fine_index):
+    padded = padded_2(features, (("sx", 0), ("sy", 1)), REACH * SB)
+    block_x, block_y = fine_index.shape[:2]
     win = (2 * REACH + 1) * SB
     start_x = (jnp.arange(block_x, dtype=jnp.int32) * SB)[:, None, None]
     start_y = (jnp.arange(block_y, dtype=jnp.int32) * SB)[None, :, None]
-    fine_at = (start_x + fine_index // win) * side + start_y + fine_index % win
+    at = (start_x + fine_index // win) * padded.shape[1] + start_y + fine_index % win
+    return jnp.take(padded.reshape(-1, padded.shape[2]), at.reshape(-1), axis=0)
+
+
+def body(features, coarse_features, fine_index, own_order):
+    block_x, block_y, fine_count = fine_index.shape
+    blocks = block_x * block_y
+    fine, coarse, flag = exchange(features, coarse_features, fine_index.reshape(blocks, fine_count))
+    fine = lax.cond(flag[0, 0] > 0.0, lambda f: whole_tiles(features, fine_index), lambda f: f, fine)
     vmem = pl.BlockSpec(memory_space=pltpu.VMEM)
     out = pl.pallas_call(
         kernel,
@@ -204,7 +363,6 @@
         in_specs=[vmem] * 4,
         out_specs=vmem,
         scratch_shapes=[
-            pltpu.VMEM((512, 256), F32),
             pltpu.VMEM((4, 384, 256), BF16),
             pltpu.VMEM((4, 384, 128), F32),
             pltpu.VMEM((4, 128, 384), F32),
@@ -213,7 +371,7 @@
             pltpu.VMEM((4, 256, 256), F32),
         ],
         compiler_params=pltpu.CompilerParams(vmem_limit_bytes=40 * 2**20),
-    )(padded, coarse, fine_at.reshape(-1, 1), own_order.reshape(-1, 1))
+    )(features, coarse, fine, own_order.reshape(blocks, -1))
     return out.reshape(block_x, block_y, 512, 256)
 
 

time: 110 us -> 63.6 us (0.58)
  blocking collectives: 45.7 us -> 0 us
  Pallas kernels: 40 us -> 61.8 us
  waiting for transfers between devices: 11.7 us -> 0 us
  starting transfers between devices: 8.65 us -> 0 us
  other arithmetic: 2.15 us -> 0 us
    all_gather x1 -> x0, blocking collectives: 45.7 us -> none  [body(): coarse = lax.all_gather(coarse_features, ('sx', 'sy'), axis=0, tiled=True)]
    pallas_call x0 -> x1, Pallas kernels: none -> 24.6 us  [exchange(): pl.pallas_call(comm_kernel, out_shape=(jax.ShapeDtypeStruct((asked, width...]
    ppermute x4 -> x0, waiting for transfers between devices: 11.7 us -> none  [the longest x2 11.7 us: padded_2(): lax.ppermute(lax.slice_in_dim(block, block.shape[dim] - width, None, axis...]
    ppermute x4 -> x0, starting transfers between devices: 8.65 us -> none  [the longest x2 4.95 us: padded_2(): lax.ppermute(lax.slice_in_dim(block, block.shape[dim] - width, None, axis...]
    pallas_call x1, Pallas kernels: 40 us -> 37.2 us  [body(): pl.pallas_call(kernel, out_shape=jax.ShapeDtypeStruct((4, 512, 256), F32)...]
    concatenate x1 -> x0, other arithmetic: 2.07 us -> none  [padded_2(): block = jnp.concatenate([low, block, high], axis=dim)]
  transfers between devices with their start and end apart: 4 -> 0, of which waited for: 1 -> 0; matrix products, arithmetic and copies ran while one was open for 2% -> 0% of each run, Pallas kernels for 0% -> 0%
where the time goes in v3:
time: 63.6 us; the launch traced here: 63.2 us
  Pallas kernels  61.8 us (97%)
  local copies, waits for them, and re-layouts  1.18 us (2%)
    pallas_call x1, Pallas kernels, body(): pl.pallas_call(kernel, out_shape=jax.ShapeDtypeStruct((4, 512, 256), F32)...  37.2 us
    pallas_call x1, Pallas kernels, exchange(): pl.pallas_call(comm_kernel, out_shape=(jax.ShapeDtypeStruct((asked, width...  24.6 us

profile of v3, /device:TPU:1, one launch (start us, length us, event | category | flops | bytes accessed | tf_op | source)
XLA Modules:
  0.0 63.2 jit_solution(13679213943320193934)
XLA Ops:
  0.0 0.0 copy-start
  0.0 0.7 %copy-done = bf16[1,256]{1,0:T(2,128)(2,1)S(1)} copy-done((bf16[1,256]{1,0:T(2,128)(2,1)S(1)}, bf16[1,256]{1,0:T(2,128)(2,1)}, u32[]{:S(2)}) %copy-start) | copy-done | bytes 536
  0.7 24.6 %shard_map.46 = (bf16[512,256]{1,0:T(8,128)(2,1)S(1)}, bf16[128,256]{1,0:T(8,128)(2,1)S(1)}, f32[1,128]{1,0:T(1,128)S(1)}) custom-call(bf16[32,32,256]{2,1,0:T(8,128)(2,1)} %feat_ref.3, bf16[1,256]{1,0:T(2,128)(2,1)S(1)} %copy-done, s32[4,128]{1,0:T(4,128)} %bitcast.12), custom_call_target="tpu_custom_call" | custom-call | tf_op jit(solution)/shard_map/pallas_call | solution.py:298
  25.3 0.0 copy-start.2
  25.3 0.2 conditional.1
  25.5 0.5 copy-done.2
  26.0 37.2 %shard_map.47 = f32[4,512,256]{2,1,0:T(8,128)} custom-call(bf16[32,32,256]{2,1,0:T(8,128)(2,1)} %feat_ref.3, bf16[128,256]{1,0:T(8,128)(2,1)S(1)} %get-tuple-element.18.coarse_ref, bf16[512,256]{1,0:T(8,128)(2,1)S(1)} %get-tuple-element.21.fine_ref, s32[4,256]{1,0:T(4,128)S(1)} %reshape.64.own_at_ref), custom_call_target="tpu_custom_call" | custom-call | tf_op jit(solution)/shard_map/pallas_call | solution.py:360
  (1 shorter events, 0.0 us)
Async XLA Ops:
  0.0 0.7 %copy-start = (bf16[1,256]{1,0:T(2,128)(2,1)S(1)}, bf16[1,256]{1,0:T(2,128)(2,1)}, u32[]{:S(2)}) copy-start(bf16[1,256]{1,0:T(2,128)(2,1)} %coarse_ref.1) | copy-start | bytes 1540
  25.3 0.7 %copy-start.2 = (s32[2,2,256]{2,1,0:T(2,128)S(1)}, s32[2,2,256]{2,1,0:T(2,128)}, u32[]{:S(2)}) copy-start(s32[2,2,256]{2,1,0:T(2,128)} %param.9) | copy-start | bytes 12292

commit v4 on v3

--- a/solution.py
+++ b/solution.py
@@ -11,23 +11,42 @@
 BS = 32
 F32 = jnp.float32
 BF16 = jnp.bfloat16
-HI = lax.Precision.HIGHEST
 NN = (((1,), (0,)), ((), ()))
 NT = (((1,), (1,)), ((), ()))
 MESH = pl.DeviceIdType.MESH
 
 
-def mm(a, b, dims=NN):
-    return lax.dot_general(a, b, dims, precision=HI, preferred_element_type=F32)
-
-
 def bmm(a, b, dims=NN):
     return lax.dot_general(a, b, dims, preferred_element_type=F32)
+
+
+def split(x):
+    hi = x.astype(BF16)
+    rest = x - hi.astype(F32)
+    mid = rest.astype(BF16)
+    return hi, mid, (rest - mid.astype(F32)).astype(BF16)
+
+
+def mm(a, b, dims=NN):
+    (ca,), (cb,) = dims[0]
+    a1, a2, a3 = split(a)
+    b1, b2, b3 = split(b)
+    return bmm(jnp.concatenate([a1, a1, a2, a2, a1, a3], ca), jnp.concatenate([b1, b2, b1, b2, b3, b1], cb), dims)
 
 
 def lane_pick(x, lane):
     at = (lax.broadcasted_iota(jnp.int32, x.shape, 1) // BS) * BS + lane
     return jnp.take_along_axis(x, at, axis=1)
+
+
+def sub_pick(x, q):
+    return jnp.broadcast_to(x[q : q + 1], (8, 128))
+
+
+def total(terms):
+    while len(terms) > 1:
+        terms = [sum(terms[k : k + 2][1:], terms[k]) for k in range(0, len(terms), 2)]
+    return terms[0]
 
 
 def base_block(z):
@@ -35,29 +54,32 @@
     li = lax.broadcasted_iota(jnp.int32, (8, 128), 1) % BS
     si = lax.broadcasted_iota(jnp.int32, (8, 128), 0)
     factor = []
-    for g in range(4):
-        cols = [[lane_pick(vs[v], 8 * g + q) for v in range(4)] for q in range(8)]
-        here = li // 8 == g
-        eye = (li % 8 == si).astype(F32)
-        vs = [jnp.where(here, eye if v == g else 0.0, vs[v]) for v in range(4)]
-        rows = jnp.zeros((8, 128), F32)
-        for q in range(8):
-            piv = jnp.broadcast_to(cols[q][g][q : q + 1], (8, 128))
+    for h in range(2):
+        group = (2 * h, 2 * h + 1)
+        cols = [[lane_pick(vs[v], 16 * h + q) for v in range(4)] for q in range(16)]
+        vs = [
+            jnp.where(li // 16 == h, (li == si + 8 * v).astype(F32) if v in group else 0.0, vs[v]) for v in range(4)
+        ]
+        rows = [jnp.zeros((8, 128), F32)] * 2
+        piv = sub_pick(cols[0][2 * h], 0)
+        for q in range(16):
+            g, sq = group[q // 8], q % 8
             rinv = 1.0 / piv
-            plain = jnp.broadcast_to(vs[g][q : q + 1], (8, 128))
-            rows = jnp.where(si == q, plain * lax.rsqrt(piv), rows)
-            row = plain * rinv
-            later = {p: jnp.broadcast_to(cols[p][g][q : q + 1], (8, 128)) * rinv for p in range(q + 1, 8)}
-            for v in range(4):
+            plain = sub_pick(vs[g], sq)
+            rows[q // 8] = jnp.where(si == sq, plain * lax.rsqrt(piv), rows[q // 8])
+            later = {p: sub_pick(cols[p][g], sq) for p in range(q + 1, 16)}
+            if q < 15:
+                piv = sub_pick(cols[q + 1][group[(q + 1) // 8]], (q + 1) % 8) - later[q + 1] * later[q + 1] * rinv
+            for v in group:
                 m = cols[q][v]
-                vs[v] = vs[v] - m * row
+                m = (jnp.where(si == sq, m - 1.0, m) if v == g else m) * rinv
+                vs[v] = vs[v] - m * plain
                 for p in later:
                     cols[p][v] = cols[p][v] - m * later[p]
-                if v == g:
-                    vs[v] = jnp.where(si == q, row, vs[v])
-                    for p in later:
-                        cols[p][v] = jnp.where(si == q, later[p], cols[p][v])
-        factor.append(jnp.where(li <= si + 8 * g, rows, 0.0))
+        for v in range(4):
+            if v not in group:
+                vs[v] = vs[v] - total([cols[q][v] * sub_pick(vs[group[q // 8]], q % 8) for q in range(16)])
+        factor += [jnp.where(li <= si + 8 * group[k], rows[k], 0.0) for k in range(2)]
     return jnp.concatenate(vs, 0), jnp.concatenate(factor, 0)
 
 
@@ -65,30 +87,34 @@
     return jnp.where(diag, jnp.concatenate([x] * 4, 0), 0.0)
 
 
-def inner(zp):
+def cut(x, i, u):
+    return x[BS * i : BS * i + BS, BS * u : BS * u + BS]
+
+
+def inner(blocks, hook):
     diag = lax.broadcasted_iota(jnp.int32, (128, 128), 0) // BS == lax.broadcasted_iota(jnp.int32, (128, 128), 1) // BS
-    zp = [[z[BS * t : BS * t + BS] for t in range(4)] for z in zp]
-    out = []
+    zp = [[None] * 4 for _ in range(4)]
+    for u in range(4):
+        for i in range(4):
+            zp[u][i] = jnp.concatenate([cut(b, i, u) for b in blocks], 1)
+    factor = [[] for _ in blocks]
     for t in range(4):
+        hook(t)
         dinv, w = base_block(zp[t][t])
         src = [spread(zp[u][t], diag) if u != t else None for u in range(4)]
-        out.append([mm(w, src[u]) for u in range(t)] + [w] + [jnp.zeros_like(w)] * (3 - t))
-        dspread = spread(dinv, diag)
-        for i in range(t + 1, 4):
-            g = mm(zp[t][i], dspread)
-            for u in range(4):
-                zp[u][i] = -g if u == t else zp[u][i] - mm(g, src[u])
-    return out
-
-
-def unpack(out, s):
-    return jnp.concatenate(
-        [jnp.concatenate([out[t][u][:, BS * s : BS * s + BS] for u in range(4)], 1) for t in range(4)], 0
-    )
-
-
-def pack(blocks):
-    return [jnp.concatenate([b[:, BS * u : BS * u + BS] for b in blocks], 1) for u in range(4)]
+        if t < 3:
+            g = mm(jnp.concatenate(zp[t][t + 1 :], 0), spread(dinv, diag))
+            for u in sorted(range(4), key=lambda u: u != t + 1):
+                change = g if u == t else mm(g, src[u])
+                for i in range(t + 1, 4):
+                    x = change[BS * (i - t - 1) : BS * (i - t)]
+                    zp[u][i] = -x if u == t else zp[u][i] - x
+        row = [mm(w, src[u]) for u in range(t)] + [w]
+        for s in range(len(blocks)):
+            parts = [x[:, BS * s : BS * s + BS] for x in row]
+            parts += [jnp.zeros((BS, BS * (3 - t)), F32)] if t < 3 else []
+            factor[s].append(jnp.concatenate(parts, 1))
+    return [jnp.concatenate(f, 0) for f in factor]
 
 
 def squares(x):
@@ -101,11 +127,11 @@
     return jnp.sum(x2, axis=1, keepdims=True), row
 
 
-def theta(a, b, sa, sb, same):
+def theta(a, b, sa, sb, shift=None):
     t = jnp.exp((2.0 * bmm(a, b, NT) - (sa + sb)) * (1.0 / a.shape[1]))
-    if same:
+    if shift is not None:
         i, j = lax.broadcasted_iota(jnp.int32, t.shape, 0), lax.broadcasted_iota(jnp.int32, t.shape, 1)
-        t = jnp.where(i == j, 1.0 + NUGGET, t)
+        t = jnp.where(i + shift == j, 1.0 + NUGGET, t)
     return t
 
 
@@ -115,57 +141,71 @@
     return jnp.concatenate([x, pad], 0).T
 
 
-def kernel(feat_ref, coarse_ref, fine_ref, own_at_ref, out_ref, fo_ref, k_ref, kt_ref, a_ref, lof_ref, e_ref):
+def kernel(feat_ref, coarse_ref, fine_ref, own_at_ref, out_ref, p_ref, k_ref, kt_ref, th_ref, e_ref):
     width = feat_ref.shape[2]
-    nf = 128
+    n = 128
+    four = range(4)
     pc = coarse_ref[...]
     sc_col, sc_row = squares(pc)
     own_at = column(own_at_ref[...])
     lane = lax.broadcasted_iota(jnp.int32, (256, 256), 1).astype(F32)
-    for s in range(4):
+
+    def kernel_matrix(s):
         bx, by = divmod(s, 2)
         own = feat_ref[SB * bx : SB * bx + SB, SB * by : SB * by + SB].reshape(256, width)
         hot = jnp.where(lane == own_at[:, s : s + 1], 1.0, 0.0).astype(BF16)
-        fo_ref[s, nf:] = bmm(hot, own).astype(BF16)
-        fo_ref[s, :nf] = fine_ref[nf * s : nf * s + nf]
-    acc = theta(pc, pc, sc_col, sc_row, True)
-    wc = unpack(inner(pack([acc] * 4)), 0)
-    wct = wc.T
-    for s in range(4):
-        p = fo_ref[s]
+        p_ref[s, n:] = bmm(hot, own).astype(BF16)
+        p_ref[s, :n] = fine_ref[n * s : n * s + n]
+        p = p_ref[s]
         col, row = squares(p)
-        kc = mm(theta(p, pc, col, sc_row, False), wc, NT)
-        k_ref[s] = kc
-        kt_ref[s] = mm(wc, theta(pc, p, sc_col, row, False))
-        a_ref[s] = theta(p, p, col, row, True) - mm(kc, kc, NT)
-    out = inner(pack([a_ref[s, :nf, :nf] for s in range(4)]))
-    for s in range(4):
-        wf = unpack(out, s)
-        lof = mm(a_ref[s, nf:, :nf], wf, NT)
-        lof_ref[s] = lof
-        a_ref[s, nf:, nf:] = a_ref[s, nf:, nf:] - mm(lof, lof, NT)
-        qft = mm(wf.T, mm(wf, a_ref[s, :nf, nf:]))
-        e_ref[s, 128:256] = -qft
-        e_ref[s, :128] = mm(wct, mm(kt_ref[s, :, :nf], qft) - kt_ref[s, :, nf:])
-    out = inner(pack([a_ref[s, 128:256, 128:256] for s in range(4)]))
-    for s in range(4):
-        w0 = unpack(out, s)
-        l10 = mm(a_ref[s, 256:, 128:256], w0, NT)
-        lof_ref[s, :128] = l10
-        a_ref[s, 256:, 256:] = a_ref[s, 256:, 256:] - mm(l10, l10, NT)
-        top = mm(e_ref[s, :, :128], w0, NT)
-        w0t = w0.T
-        out_ref[s, :256, :128] = top
-        out_ref[s, 256:384, :128] = w0t
-        out_ref[s, 384:, :128] = jnp.zeros((128, 128), F32)
-        e_ref[s, :, 128:] = e_ref[s, :, 128:] - mm(top, l10, NT)
-        a_ref[s, :128, :128] = mm(w0t, l10, NT)
-    out = inner(pack([a_ref[s, 256:, 256:] for s in range(4)]))
-    for s in range(4):
-        w1 = unpack(out, s)
-        out_ref[s, :256, 128:] = mm(e_ref[s, :, 128:], w1, NT)
-        out_ref[s, 256:384, 128:] = -mm(a_ref[s, :128, :128], w1, NT)
-        out_ref[s, 384:, 128:] = w1.T
+        k_ref[s] = theta(p, pc, col, sc_row)
+        kt_ref[s] = theta(pc, p, sc_col, row)
+        th_ref[s, :, :n] = theta(p, p[:n], col, row[:, :n], 0)
+        th_ref[s, n : 2 * n, n : 2 * n] = theta(p[n : 2 * n], p[n : 2 * n], col[n : 2 * n], row[:, n : 2 * n], 0)
+        th_ref[s, 2 * n :, n:] = theta(p[2 * n :], p[n:], col[2 * n :], row[:, n:], n)
+
+    wc = inner([theta(pc, pc, sc_col, sc_row, 0)] * 4, kernel_matrix)[0]
+
+    kf = mm(jnp.concatenate([k_ref[s, :n] for s in four], 0), wc, NT)
+    kf = [kf[n * s : n * s + n] for s in four]
+
+    def leave_coarse(s):
+        ko = mm(k_ref[s, n:], wc, NT)
+        th_ref[s, n:, :n] = th_ref[s, n:, :n] - mm(ko, kf[s], NT)
+        th_ref[s, n : 2 * n, n : 2 * n] = th_ref[s, n : 2 * n, n : 2 * n] - mm(ko[:n], ko[:n], NT)
+        th_ref[s, 2 * n :, n:] = th_ref[s, 2 * n :, n:] - mm(ko[n:], ko, NT)
+
+    wf = inner([th_ref[s, :n, :n] - mm(kf[s], kf[s], NT) for s in four], leave_coarse)
+
+    lof = [mm(th_ref[s, n : 2 * n, :n], wf[s], NT) for s in four]
+    cinv = mm(wc.T, wc)
+
+    def leave_fine(s):
+        low = mm(th_ref[s, 2 * n :, :n], wf[s], NT)
+        both = jnp.concatenate([lof[s], low], 0)
+        th_ref[s, 2 * n :, n:] = th_ref[s, 2 * n :, n:] - mm(low, both, NT)
+        qt = mm(both, wf[s]).T
+        ht = mm(cinv, kt_ref[s])
+        e_ref[s, :n] = mm(ht[:, :n], qt) - ht[:, n:]
+        e_ref[s, n : 2 * n] = -qt
+
+    w0 = inner([th_ref[s, n : 2 * n, n : 2 * n] - mm(lof[s], lof[s], NT) for s in four], leave_fine)
+
+    l10 = [mm(th_ref[s, 2 * n :, n : 2 * n], w0[s], NT) for s in four]
+
+    def first_half(s):
+        top = mm(e_ref[s, : 2 * n, :n], w0[s], NT)
+        w0t = w0[s].T
+        out_ref[s, : 2 * n, :n] = top
+        out_ref[s, 2 * n : 3 * n, :n] = w0t
+        out_ref[s, 3 * n :, :n] = jnp.zeros((n, n), F32)
+        e_ref[s, : 2 * n, n:] = e_ref[s, : 2 * n, n:] - mm(top, l10[s], NT)
+        e_ref[s, 2 * n :, n:] = -mm(w0t, l10[s], NT)
+
+    w1 = inner([th_ref[s, 2 * n :, 2 * n :] - mm(l10[s], l10[s], NT) for s in four], first_half)
+    for s in four:
+        out_ref[s, : 3 * n, n:] = mm(e_ref[s, :, n:], w1[s], NT)
+        out_ref[s, 3 * n :, n:] = w1[s].T
 
 
 OFFS = ((-1, -1), (-1, 0), (-1, 1), (0, -1), (0, 1), (1, -1), (1, 0), (1, 1))
@@ -367,8 +407,7 @@
             pltpu.VMEM((4, 384, 128), F32),
             pltpu.VMEM((4, 128, 384), F32),
             pltpu.VMEM((4, 384, 384), F32),
-            pltpu.VMEM((4, 256, 128), F32),
-            pltpu.VMEM((4, 256, 256), F32),
+            pltpu.VMEM((4, 384, 256), F32),
         ],
         compiler_params=pltpu.CompilerParams(vmem_limit_bytes=40 * 2**20),
     )(features, coarse, fine, own_order.reshape(blocks, -1))

time: 63.6 us -> 48.4 us (0.76)
  Pallas kernels: 61.8 us -> 46.6 us
    pallas_call x1, Pallas kernels: 37.2 us -> 22 us  [body(): pl.pallas_call(kernel, out_shape=jax.ShapeDtypeStruct((4, 512, 256), F32)...]
where the time goes in v4:
time: 48.4 us; the launch traced here: 48 us
  Pallas kernels  46.6 us (96%)
  local copies, waits for them, and re-layouts  1.18 us (2%)
    pallas_call x1, Pallas kernels, exchange(): pl.pallas_call(comm_kernel, out_shape=(jax.ShapeDtypeStruct((asked, width...  24.6 us
    pallas_call x1, Pallas kernels, body(): pl.pallas_call(kernel, out_shape=jax.ShapeDtypeStruct((4, 512, 256), F32)...  22 us
    unnamed x4, local copies, waits for them, and re-layouts  1.17 us

profile of v4, /device:TPU:1, one launch (start us, length us, event | category | flops | bytes accessed | tf_op | source)
XLA Modules:
  0.0 48.0 jit_solution(11388617353809641053)
XLA Ops:
  0.0 0.0 copy-start
  0.0 0.7 %copy-done = bf16[1,256]{1,0:T(2,128)(2,1)S(1)} copy-done((bf16[1,256]{1,0:T(2,128)(2,1)S(1)}, bf16[1,256]{1,0:T(2,128)(2,1)}, u32[]{:S(2)}) %copy-start) | copy-done | bytes 536
  0.7 24.6 %shard_map.46 = (bf16[512,256]{1,0:T(8,128)(2,1)S(1)}, bf16[128,256]{1,0:T(8,128)(2,1)S(1)}, f32[1,128]{1,0:T(1,128)S(1)}) custom-call(bf16[32,32,256]{2,1,0:T(8,128)(2,1)} %feat_ref.3, bf16[1,256]{1,0:T(2,128)(2,1)S(1)} %copy-done, s32[4,128]{1,0:T(4,128)} %bitcast.12), custom_call_target="tpu_custom_call" | custom-call | tf_op jit(solution)/shard_map/pallas_call | solution.py:338
  25.3 0.0 copy-start.2
  25.3 0.2 conditional.1
  25.5 0.5 %copy-done.2 = s32[2,2,256]{2,1,0:T(2,128)S(1)} copy-done((s32[2,2,256]{2,1,0:T(2,128)S(1)}, s32[2,2,256]{2,1,0:T(2,128)}, u32[]{:S(2)}) %copy-start.2) | copy-done | bytes 4120
  26.0 22.0 %shard_map.47 = f32[4,512,256]{2,1,0:T(8,128)} custom-call(bf16[32,32,256]{2,1,0:T(8,128)(2,1)} %feat_ref.3, bf16[128,256]{1,0:T(8,128)(2,1)S(1)} %get-tuple-element.18.coarse_ref, bf16[512,256]{1,0:T(8,128)(2,1)S(1)} %get-tuple-element.21.fine_ref, s32[4,256]{1,0:T(4,128)S(1)} %reshape.64.own_at_ref), custom_call_target="tpu_custom_call" | custom-call | tf_op jit(solution)/shard_map/pallas_call | solution.py:400
  (1 shorter events, 0.0 us)
Async XLA Ops:
  0.0 0.7 %copy-start = (bf16[1,256]{1,0:T(2,128)(2,1)S(1)}, bf16[1,256]{1,0:T(2,128)(2,1)}, u32[]{:S(2)}) copy-start(bf16[1,256]{1,0:T(2,128)(2,1)} %coarse_ref.1) | copy-start | bytes 1540
  25.3 0.7 %copy-start.2 = (s32[2,2,256]{2,1,0:T(2,128)S(1)}, s32[2,2,256]{2,1,0:T(2,128)}, u32[]{:S(2)}) copy-start(s32[2,2,256]{2,1,0:T(2,128)} %param.9) | copy-start | bytes 12292

commit v5 on v4

--- a/solution.py
+++ b/solution.py
@@ -20,18 +20,11 @@
     return lax.dot_general(a, b, dims, preferred_element_type=F32)
 
 
-def split(x):
-    hi = x.astype(BF16)
-    rest = x - hi.astype(F32)
-    mid = rest.astype(BF16)
-    return hi, mid, (rest - mid.astype(F32)).astype(BF16)
-
-
 def mm(a, b, dims=NN):
     (ca,), (cb,) = dims[0]
-    a1, a2, a3 = split(a)
-    b1, b2, b3 = split(b)
-    return bmm(jnp.concatenate([a1, a1, a2, a2, a1, a3], ca), jnp.concatenate([b1, b2, b1, b2, b3, b1], cb), dims)
+    a1, b1 = a.astype(BF16), b.astype(BF16)
+    a2, b2 = (a - a1.astype(F32)).astype(BF16), (b - b1.astype(F32)).astype(BF16)
+    return bmm(jnp.concatenate([a1, a1, a2], ca), jnp.concatenate([b1, b2, b1], cb), dims)
 
 
 def lane_pick(x, lane):
@@ -208,14 +201,16 @@
         out_ref[s, 3 * n :, n:] = w1[s].T
 
 
-OFFS = ((-1, -1), (-1, 0), (-1, 1), (0, -1), (0, 1), (1, -1), (1, 0), (1, 1))
+OFFS = ((-1, -1), (-1, 1), (1, -1), (1, 1), (-1, 0), (0, -1), (0, 1), (1, 0))
+BACK = (3, 2, 1, 0, 7, 6, 5, 4)
+SIDE = 4
 CAPS = tuple(112 if 0 in o else 96 for o in OFFS)
 STARTS = tuple(sum(CAPS[:n]) for n in range(9))
 
 
 def comm_kernel(
     feat_ref, coarse_ref, fine_at_ref, fine_ref, coarse_out_ref, flag_ref,
-    tile_ref, row_ref, all_ref, code_ref, codes_ref, out_ref, in_ref,
+    tile_ref, row_ref, line_ref, all_ref, code_ref, codes_ref, out_ref, in_ref,
     a_send, a_recv, b_send, b_recv, c_send, c_recv, d_send, d_recv, tile_sem,
 ):
     nx, ny = lax.axis_size("sx"), lax.axis_size("sy")
@@ -237,8 +232,11 @@
     load = pltpu.make_async_copy(feat_ref, tile_ref, tile_sem)
     load.start()
     barrier = pltpu.get_barrier_semaphore()
-    partners = [(dx, dy) for dx, dy in OFFS if dx and dy]
-    partners += [(0, k) for k in range(1, ny)] + [(k, 0) for k in range(1, nx)]
+    x, y = i // SIDE, lax.rem(i, SIDE)
+    along_y = [lax.rem(y + k, SIDE) - y for k in range(1, SIDE)]
+    along_x = [SIDE * k for k in range(1, nx // SIDE)]
+    partners = [(dx, dy) for dx, dy in OFFS if dx]
+    partners += [(0, k) for k in range(1, ny)] + [(k, 0) for k in along_y] + [(k, 0) for k in along_x]
     for dx, dy in partners:
         pl.semaphore_signal(barrier, inc=1, device_id=at(dx, dy), device_id_type=MESH)
 
@@ -280,12 +278,12 @@
     pl.semaphore_wait(barrier, len(partners))
 
     asks = [
-        send(code_ref, codes_ref.at[pl.ds(7 - n, 1)], c_send.at[n], c_recv.at[7 - n], at(*OFFS[n])) for n in range(8)
+        send(code_ref, codes_ref.at[pl.ds(BACK[n], 1)], c_send.at[n], c_recv.at[BACK[n]], at(*OFFS[n])) for n in range(8)
     ]
     stage_a = [
-        send(row_ref, all_ref.at[i, pl.ds(j, 1)], a_send.at[k], a_recv.at[k], at(0, k)) for k in range(1, ny)
+        send(row_ref, line_ref.at[pl.ds(j, 1)], a_send.at[k], a_recv.at[k], at(0, k)) for k in range(1, ny)
     ]
-    all_ref[i, pl.ds(j, 1)] = row_ref[...]
+    line_ref[pl.ds(j, 1)] = row_ref[...]
     load.wait()
     tile = tile_ref[...].reshape(cells, width)
     lane = lax.broadcasted_iota(jnp.int32, (asked, cells), 1).astype(F32)
@@ -298,34 +296,39 @@
     rank = jnp.where(ok, rank, -1.0)
     for copy in stage_a:
         copy.wait()
-    stage_b = [send(all_ref.at[i], all_ref.at[i], b_send.at[k], b_recv.at[k], at(k, 0)) for k in range(1, nx)]
+    all_ref[i] = line_ref[...].reshape(ny, width + 128).astype(BF16)
+    stage_b = [
+        send(all_ref.at[i], all_ref.at[i], b_send.at[k], b_recv.at[k], at(step, 0)) for k, step in enumerate(along_y)
+    ]
     moves = []
-    for n in (0, 2, 5, 7, 1, 6, 3, 4):
-        cap = CAPS[n]
-        slots = lax.broadcasted_iota(jnp.int32, (cap, asked), 0).astype(F32)
-        cell = jnp.sum(jnp.where(slots == rank[n : n + 1], offset[n : n + 1], 0.0), axis=1, keepdims=True)
-        hot = jnp.where(lane[:cap] == cell, 1.0, 0.0).astype(BF16)
-        out_ref[STARTS[n] : STARTS[n + 1]] = bmm(hot, tile).astype(BF16)
-        moves.append(
-            send(
-                out_ref.at[pl.ds(STARTS[n], cap)],
-                in_ref.at[pl.ds(STARTS[7 - n], cap)],
-                d_send.at[n],
-                d_recv.at[7 - n],
-                at(*OFFS[n]),
-            )
-        )
+    for group in ((0, 1, 2, 3), (4, 5, 6, 7)):
+        hot = []
+        for n in group:
+            slots = lax.broadcasted_iota(jnp.int32, (CAPS[n], asked), 0).astype(F32)
+            cell = jnp.sum(jnp.where(slots == rank[n : n + 1], offset[n : n + 1], 0.0), axis=1, keepdims=True)
+            hot.append(jnp.where(lane[: CAPS[n]] == cell, 1.0, 0.0).astype(BF16))
+        low, high = STARTS[group[0]], STARTS[group[-1] + 1]
+        out_ref[low:high] = bmm(jnp.concatenate(hot, 0), tile).astype(BF16)
+        for n in group:
+            src = out_ref.at[pl.ds(STARTS[n], CAPS[n])]
+            dst = in_ref.at[pl.ds(STARTS[BACK[n]], CAPS[n])]
+            moves.append(send(src, dst, d_send.at[n], d_recv.at[BACK[n]], at(*OFFS[n])))
     for copy in stage_b:
         copy.wait()
-    full = all_ref[...].reshape(nx * ny, width + 128)
+    lines = all_ref.at[pl.ds(SIDE * x, SIDE)]
+    stage_c = [
+        send(lines, lines, b_send.at[SIDE + k], b_recv.at[SIDE + k], at(step, 0)) for k, step in enumerate(along_x)
+    ]
+    lane = lax.broadcasted_iota(jnp.int32, (asked, STARTS[8]), 1).astype(F32)
+    hot = jnp.where(lane == where_at[:, :1], 1.0, 0.0).astype(BF16)
+    for copy in moves:
+        copy.wait()
+    fine_ref[...] = (fine + bmm(hot, in_ref[...])).astype(BF16)
+    for copy in stage_c:
+        copy.wait()
+    full = all_ref[...].astype(F32).reshape(nx * ny, width + 128)
     coarse_out_ref[...] = full[:, :width].astype(BF16)
     flag_ref[...] = jnp.sum(full[:, width:], axis=0, keepdims=True)
-    for copy in moves:
-        copy.wait()
-    got = in_ref[...]
-    lane = lax.broadcasted_iota(jnp.int32, (asked, got.shape[0]), 1).astype(F32)
-    fine = fine + bmm(jnp.where(lane == where_at[:, :1], 1.0, 0.0).astype(BF16), got)
-    fine_ref[...] = fine.astype(BF16)
 
 
 def exchange(features, coarse_features, fine_at):
@@ -347,15 +350,16 @@
         scratch_shapes=[
             pltpu.VMEM((rows, cols, width), BF16),
             pltpu.VMEM((1, 1, width + 128), F32),
-            pltpu.VMEM((nx, ny, 1, width + 128), F32),
+            pltpu.VMEM((ny, 1, width + 128), F32),
+            pltpu.VMEM((nx, ny, width + 128), BF16),
             pltpu.VMEM((1, 1, asked), F32),
             pltpu.VMEM((8, 1, asked), F32),
             pltpu.VMEM((STARTS[8], width), BF16),
             pltpu.VMEM((STARTS[8], width), BF16),
             dma((ny,)),
             dma((ny,)),
-            dma((nx,)),
-            dma((nx,)),
+            dma((2 * SIDE,)),
+            dma((2 * SIDE,)),
             dma((8,)),
             dma((8,)),
             dma((8,)),

time: 48.4 us -> 45.3 us (0.936)
  Pallas kernels: 46.6 us -> 43.6 us
    pallas_call x1, Pallas kernels: 22 us -> 20.4 us  [body(): pl.pallas_call(kernel, out_shape=jax.ShapeDtypeStruct((4, 512, 256), F32)...]
    pallas_call x1, Pallas kernels: 24.6 us -> 23.2 us  [exchange(): pl.pallas_call(comm_kernel, out_shape=(jax.ShapeDtypeStruct((asked, width...]
where the time goes in v5:
time: 45.3 us; the launch traced here: 45 us
  Pallas kernels  43.6 us (96%)
  local copies, waits for them, and re-layouts  1.18 us (3%)
    pallas_call x1, Pallas kernels, exchange(): pl.pallas_call(comm_kernel, out_shape=(jax.ShapeDtypeStruct((asked, width...  23.2 us
    pallas_call x1, Pallas kernels, body(): pl.pallas_call(kernel, out_shape=jax.ShapeDtypeStruct((4, 512, 256), F32)...  20.4 us
    unnamed x4, local copies, waits for them, and re-layouts  1.17 us

profile of v5, /device:TPU:1, one launch (start us, length us, event | category | flops | bytes accessed | tf_op | source)
XLA Modules:
  0.0 45.0 jit_solution(4768339881722589880)
XLA Ops:
  0.0 0.0 copy-start
  0.0 0.7 %copy-done = bf16[1,256]{1,0:T(2,128)(2,1)S(1)} copy-done((bf16[1,256]{1,0:T(2,128)(2,1)S(1)}, bf16[1,256]{1,0:T(2,128)(2,1)}, u32[]{:S(2)}) %copy-start) | copy-done | bytes 536
  0.7 23.2 %shard_map.46 = (bf16[512,256]{1,0:T(8,128)(2,1)S(1)}, bf16[128,256]{1,0:T(8,128)(2,1)S(1)}, f32[1,128]{1,0:T(1,128)S(1)}) custom-call(bf16[32,32,256]{2,1,0:T(8,128)(2,1)} %feat_ref.3, bf16[1,256]{1,0:T(2,128)(2,1)S(1)} %copy-done, s32[4,128]{1,0:T(4,128)} %bitcast.12), custom_call_target="tpu_custom_call" | custom-call | tf_op jit(solution)/shard_map/pallas_call | solution.py:341
  23.9 0.0 copy-start.2
  23.9 0.2 conditional.1
  24.1 0.5 %copy-done.2 = s32[2,2,256]{2,1,0:T(2,128)S(1)} copy-done((s32[2,2,256]{2,1,0:T(2,128)S(1)}, s32[2,2,256]{2,1,0:T(2,128)}, u32[]{:S(2)}) %copy-start.2) | copy-done | bytes 4120
  24.6 20.4 %shard_map.47 = f32[4,512,256]{2,1,0:T(8,128)} custom-call(bf16[32,32,256]{2,1,0:T(8,128)(2,1)} %feat_ref.3, bf16[128,256]{1,0:T(8,128)(2,1)S(1)} %get-tuple-element.18.coarse_ref, bf16[512,256]{1,0:T(8,128)(2,1)S(1)} %get-tuple-element.21.fine_ref, s32[4,256]{1,0:T(4,128)S(1)} %reshape.64.own_at_ref), custom_call_target="tpu_custom_call" | custom-call | tf_op jit(solution)/shard_map/pallas_call | solution.py:404
  (1 shorter events, 0.0 us)
Async XLA Ops:
  0.0 0.7 %copy-start = (bf16[1,256]{1,0:T(2,128)(2,1)S(1)}, bf16[1,256]{1,0:T(2,128)(2,1)}, u32[]{:S(2)}) copy-start(bf16[1,256]{1,0:T(2,128)(2,1)} %coarse_ref.1) | copy-start | bytes 1540
  23.9 0.7 %copy-start.2 = (s32[2,2,256]{2,1,0:T(2,128)S(1)}, s32[2,2,256]{2,1,0:T(2,128)}, u32[]{:S(2)}) copy-start(s32[2,2,256]{2,1,0:T(2,128)} %param.9) | copy-start | bytes 12292

commit v6 on v5

--- a/solution.py
+++ b/solution.py
@@ -84,14 +84,18 @@
     return x[BS * i : BS * i + BS, BS * u : BS * u + BS]
 
 
-def inner(blocks, hook):
+def inner(start, blocks, hook):
     diag = lax.broadcasted_iota(jnp.int32, (128, 128), 0) // BS == lax.broadcasted_iota(jnp.int32, (128, 128), 1) // BS
     zp = [[None] * 4 for _ in range(4)]
-    for u in range(4):
-        for i in range(4):
-            zp[u][i] = jnp.concatenate([cut(b, i, u) for b in blocks], 1)
-    factor = [[] for _ in blocks]
+    zp[0][0] = jnp.concatenate(start, 1)
+    factor = [[] for _ in start]
     for t in range(4):
+        if t == 0:
+            full = blocks()
+            for u in range(4):
+                for i in range(4):
+                    if u or i:
+                        zp[u][i] = jnp.concatenate([cut(b, i, u) for b in full], 1)
         hook(t)
         dinv, w = base_block(zp[t][t])
         src = [spread(zp[u][t], diag) if u != t else None for u in range(4)]
@@ -103,7 +107,7 @@
                     x = change[BS * (i - t - 1) : BS * (i - t)]
                     zp[u][i] = -x if u == t else zp[u][i] - x
         row = [mm(w, src[u]) for u in range(t)] + [w]
-        for s in range(len(blocks)):
+        for s in range(4):
             parts = [x[:, BS * s : BS * s + BS] for x in row]
             parts += [jnp.zeros((BS, BS * (3 - t)), F32)] if t < 3 else []
             factor[s].append(jnp.concatenate(parts, 1))
@@ -134,13 +138,25 @@
     return jnp.concatenate([x, pad], 0).T
 
 
-def kernel(feat_ref, coarse_ref, fine_ref, own_at_ref, out_ref, p_ref, k_ref, kt_ref, th_ref, e_ref):
+def kernel(
+    feat_hbm, coarse_ref, fine_ref, own_hbm, out_hbm,
+    p_ref, k_ref, kt_ref, th_ref, e_ref, feat_ref, own_ref, lo_ref, hi_ref, in_sem, lo_sem, hi_sem,
+):
+    loads = [
+        pltpu.make_async_copy(own_hbm, own_ref, in_sem.at[0]),
+        pltpu.make_async_copy(feat_hbm, feat_ref, in_sem.at[1]),
+    ]
+    for load in loads:
+        load.start()
     width = feat_ref.shape[2]
     n = 128
     four = range(4)
     pc = coarse_ref[...]
     sc_col, sc_row = squares(pc)
-    own_at = column(own_at_ref[...])
+    acc = theta(pc, pc, sc_col, sc_row, 0)
+    for load in loads:
+        load.wait()
+    own_at = column(jnp.concatenate([own_ref[0], own_ref[1]], 0))
     lane = lax.broadcasted_iota(jnp.int32, (256, 256), 1).astype(F32)
 
     def kernel_matrix(s):
@@ -157,10 +173,18 @@
         th_ref[s, n : 2 * n, n : 2 * n] = theta(p[n : 2 * n], p[n : 2 * n], col[n : 2 * n], row[:, n : 2 * n], 0)
         th_ref[s, 2 * n :, n:] = theta(p[2 * n :], p[n:], col[2 * n :], row[:, n:], n)
 
-    wc = inner([theta(pc, pc, sc_col, sc_row, 0)] * 4, kernel_matrix)[0]
-
-    kf = mm(jnp.concatenate([k_ref[s, :n] for s in four], 0), wc, NT)
-    kf = [kf[n * s : n * s + n] for s in four]
+    wc = inner([cut(acc, 0, 0)] * 4, lambda: [acc] * 4, kernel_matrix)[0]
+
+    def leading(rows, s, at):
+        own = rows[BS * s : BS * s + BS]
+        return th_ref[s, at : at + BS, at : at + BS] - mm(own, own, NT)
+
+    kf = []
+
+    def fine_block():
+        x = mm(jnp.concatenate([k_ref[s, :n] for s in four], 0), wc, NT)
+        kf.extend(x[n * s : n * s + n] for s in four)
+        return [th_ref[s, :n, :n] - mm(kf[s], kf[s], NT) for s in four]
 
     def leave_coarse(s):
         ko = mm(k_ref[s, n:], wc, NT)
@@ -168,10 +192,15 @@
         th_ref[s, n : 2 * n, n : 2 * n] = th_ref[s, n : 2 * n, n : 2 * n] - mm(ko[:n], ko[:n], NT)
         th_ref[s, 2 * n :, n:] = th_ref[s, 2 * n :, n:] - mm(ko[n:], ko, NT)
 
-    wf = inner([th_ref[s, :n, :n] - mm(kf[s], kf[s], NT) for s in four], leave_coarse)
-
-    lof = [mm(th_ref[s, n : 2 * n, :n], wf[s], NT) for s in four]
+    head = mm(jnp.concatenate([k_ref[s, :BS] for s in four], 0), wc, NT)
+    wf = inner([leading(head, s, 0) for s in four], fine_block, leave_coarse)
+
+    lof = []
     cinv = mm(wc.T, wc)
+
+    def own_block():
+        lof.extend(mm(th_ref[s, n : 2 * n, :n], wf[s], NT) for s in four)
+        return [th_ref[s, n : 2 * n, n : 2 * n] - mm(lof[s], lof[s], NT) for s in four]
 
     def leave_fine(s):
         low = mm(th_ref[s, 2 * n :, :n], wf[s], NT)
@@ -182,23 +211,36 @@
         e_ref[s, :n] = mm(ht[:, :n], qt) - ht[:, n:]
         e_ref[s, n : 2 * n] = -qt
 
-    w0 = inner([th_ref[s, n : 2 * n, n : 2 * n] - mm(lof[s], lof[s], NT) for s in four], leave_fine)
-
-    l10 = [mm(th_ref[s, 2 * n :, n : 2 * n], w0[s], NT) for s in four]
+    head = jnp.concatenate([mm(th_ref[s, n : n + BS, :n], wf[s], NT) for s in four], 0)
+    w0 = inner([leading(head, s, n) for s in four], own_block, leave_fine)
+
+    l10 = []
+    stores = []
+
+    def last_block():
+        l10.extend(mm(th_ref[s, 2 * n :, n : 2 * n], w0[s], NT) for s in four)
+        return [th_ref[s, 2 * n :, 2 * n :] - mm(l10[s], l10[s], NT) for s in four]
 
     def first_half(s):
         top = mm(e_ref[s, : 2 * n, :n], w0[s], NT)
         w0t = w0[s].T
-        out_ref[s, : 2 * n, :n] = top
-        out_ref[s, 2 * n : 3 * n, :n] = w0t
-        out_ref[s, 3 * n :, :n] = jnp.zeros((n, n), F32)
+        lo_ref[s, : 2 * n] = top
+        lo_ref[s, 2 * n : 3 * n] = w0t
+        lo_ref[s, 3 * n :] = jnp.zeros((n, n), F32)
+        stores.append(pltpu.make_async_copy(lo_ref.at[s], out_hbm.at[s, :, pl.ds(0, n)], lo_sem.at[s]))
+        stores[-1].start()
         e_ref[s, : 2 * n, n:] = e_ref[s, : 2 * n, n:] - mm(top, l10[s], NT)
         e_ref[s, 2 * n :, n:] = -mm(w0t, l10[s], NT)
 
-    w1 = inner([th_ref[s, 2 * n :, 2 * n :] - mm(l10[s], l10[s], NT) for s in four], first_half)
+    head = jnp.concatenate([mm(th_ref[s, 2 * n : 2 * n + BS, n : 2 * n], w0[s], NT) for s in four], 0)
+    w1 = inner([leading(head, s, 2 * n) for s in four], last_block, first_half)
     for s in four:
-        out_ref[s, : 3 * n, n:] = mm(e_ref[s, :, n:], w1[s], NT)
-        out_ref[s, 3 * n :, n:] = w1[s].T
+        hi_ref[s, : 3 * n] = mm(e_ref[s, :, n:], w1[s], NT)
+        hi_ref[s, 3 * n :] = w1[s].T
+        stores.append(pltpu.make_async_copy(hi_ref.at[s], out_hbm.at[s, :, pl.ds(n, n)], hi_sem.at[s]))
+        stores[-1].start()
+    for store in stores:
+        store.wait()
 
 
 OFFS = ((-1, -1), (-1, 1), (1, -1), (1, 1), (-1, 0), (0, -1), (0, 1), (1, 0))
@@ -209,9 +251,9 @@
 
 
 def comm_kernel(
-    feat_ref, coarse_ref, fine_at_ref, fine_ref, coarse_out_ref, flag_ref,
+    feat_ref, coarse_hbm, fine_at_hbm, fine_ref, coarse_out_ref, flag_ref,
     tile_ref, row_ref, line_ref, all_ref, code_ref, codes_ref, out_ref, in_ref,
-    a_send, a_recv, b_send, b_recv, c_send, c_recv, d_send, d_recv, tile_sem,
+    a_send, a_recv, b_send, b_recv, c_send, c_recv, d_send, d_recv, tile_sem, coarse_ref, fine_at_ref, in_sem,
 ):
     nx, ny = lax.axis_size("sx"), lax.axis_size("sy")
     i, j = lax.axis_index("sx"), lax.axis_index("sy")
@@ -229,6 +271,12 @@
         copy.start()
         return copy
 
+    small = [
+        pltpu.make_async_copy(fine_at_hbm, fine_at_ref, in_sem.at[0]),
+        pltpu.make_async_copy(coarse_hbm, coarse_ref, in_sem.at[1]),
+    ]
+    for copy in small:
+        copy.start()
     load = pltpu.make_async_copy(feat_ref, tile_ref, tile_sem)
     load.start()
     barrier = pltpu.get_barrier_semaphore()
@@ -240,6 +288,8 @@
     for dx, dy in partners:
         pl.semaphore_signal(barrier, inc=1, device_id=at(dx, dy), device_id_type=MESH)
 
+    for copy in small:
+        copy.wait()
     f = fine_at_ref[...]
     win_row = lax.shift_right_logical(f * 52429, 22)
     s_at = lax.broadcasted_iota(jnp.int32, f.shape, 0)
@@ -336,7 +386,7 @@
     rows, cols, width = features.shape
     asked = fine_at.shape[0] * fine_at.shape[1]
     dma = pltpu.SemaphoreType.DMA
-    hbm = pl.BlockSpec(memory_space=pl.ANY)
+    hbm = pl.BlockSpec(memory_space=pltpu.HBM)
     vmem = pl.BlockSpec(memory_space=pltpu.VMEM)
     return pl.pallas_call(
         comm_kernel,
@@ -345,7 +395,7 @@
             jax.ShapeDtypeStruct((nx * ny, width), BF16),
             jax.ShapeDtypeStruct((1, 128), F32),
         ),
-        in_specs=[hbm, vmem, vmem],
+        in_specs=[hbm, hbm, hbm],
         out_specs=(vmem, vmem, vmem),
         scratch_shapes=[
             pltpu.VMEM((rows, cols, width), BF16),
@@ -365,6 +415,9 @@
             dma((8,)),
             dma((8,)),
             dma,
+            pltpu.VMEM(coarse_features.shape, BF16),
+            pltpu.VMEM(fine_at.shape, jnp.int32),
+            dma((2,)),
         ],
         compiler_params=pltpu.CompilerParams(
             collective_id=0, has_side_effects=True, vmem_limit_bytes=32 * 2**20
@@ -401,20 +454,29 @@
     fine, coarse, flag = exchange(features, coarse_features, fine_index.reshape(blocks, fine_count))
     fine = lax.cond(flag[0, 0] > 0.0, lambda f: whole_tiles(features, fine_index), lambda f: f, fine)
     vmem = pl.BlockSpec(memory_space=pltpu.VMEM)
+    hbm = pl.BlockSpec(memory_space=pltpu.HBM)
+    dma = pltpu.SemaphoreType.DMA
     out = pl.pallas_call(
         kernel,
         out_shape=jax.ShapeDtypeStruct((4, 512, 256), F32),
-        in_specs=[vmem] * 4,
-        out_specs=vmem,
+        in_specs=[hbm, vmem, vmem, hbm],
+        out_specs=hbm,
         scratch_shapes=[
             pltpu.VMEM((4, 384, 256), BF16),
             pltpu.VMEM((4, 384, 128), F32),
             pltpu.VMEM((4, 128, 384), F32),
             pltpu.VMEM((4, 384, 384), F32),
             pltpu.VMEM((4, 384, 256), F32),
+            pltpu.VMEM(features.shape, BF16),
+            pltpu.VMEM(own_order.shape, jnp.int32),
+            pltpu.VMEM((4, 512, 128), F32),
+            pltpu.VMEM((4, 512, 128), F32),
+            dma((2,)),
+            dma((4,)),
+            dma((4,)),
         ],
         compiler_params=pltpu.CompilerParams(vmem_limit_bytes=40 * 2**20),
-    )(features, coarse, fine, own_order.reshape(blocks, -1))
+    )(features, coarse, fine, own_order)
     return out.reshape(block_x, block_y, 512, 256)
 
 

time: 45.3 us -> 44 us (0.971)
  Pallas kernels: 43.6 us -> 42.2 us
    pallas_call x1, Pallas kernels: 20.4 us -> 19.6 us  [body(): pl.pallas_call(kernel, out_shape=jax.ShapeDtypeStruct((4, 512, 256), F32)...]
    pallas_call x1, Pallas kernels: 23.2 us -> 22.5 us  [exchange(): pl.pallas_call(comm_kernel, out_shape=(jax.ShapeDtypeStruct((asked, width...]
where the time goes in v6:
time: 44 us; the launch traced here: 43.8 us
  Pallas kernels  42.2 us (96%)
  local copies, waits for them, and re-layouts  1.35 us (3%)
    pallas_call x1, Pallas kernels, exchange(): pl.pallas_call(comm_kernel, out_shape=(jax.ShapeDtypeStruct((asked, width...  22.5 us
    pallas_call x1, Pallas kernels, body(): pl.pallas_call(kernel, out_shape=jax.ShapeDtypeStruct((4, 512, 256), F32)...  19.6 us
    unnamed x4, local copies, waits for them, and re-layouts  1.35 us

profile of v6, /device:TPU:1, one launch (start us, length us, event | category | flops | bytes accessed | tf_op | source)
XLA Modules:
  0.0 43.8 jit_solution(13529337091011302624)
XLA Ops:
  0.0 0.0 copy-start.1
  0.0 0.7 %copy-done.1 = bf16[1,256]{1,0:T(2,128)(2,1)S(1)} copy-done((bf16[1,256]{1,0:T(2,128)(2,1)S(1)}, bf16[1,256]{1,0:T(2,128)(2,1)}, u32[]{:S(2)}) %copy-start.1) | copy-done | bytes 536
  0.7 22.5 %shard_map.46 = (bf16[512,256]{1,0:T(8,128)(2,1)S(1)}, bf16[128,256]{1,0:T(8,128)(2,1)S(1)}, f32[1,128]{1,0:T(1,128)S(1)}) custom-call(bf16[32,32,256]{2,1,0:T(8,128)(2,1)} %feat_hbm.1, bf16[1,256]{1,0:T(2,128)(2,1)S(1)} %copy-done.1, s32[4,128]{1,0:T(4,128)} %bitcast.12), custom_call_target="tpu_custom_call" | custom-call | tf_op jit(solution)/shard_map/pallas_call | solution.py:391
  23.2 0.0 copy-start
  23.3 0.7 %copy-done = s32[2,2,256]{2,1,0:T(2,128)S(1)} copy-done((s32[2,2,256]{2,1,0:T(2,128)S(1)}, s32[2,2,256]{2,1,0:T(2,128)}, u32[]{:S(2)}) %copy-start) | copy-done | bytes 4120
  23.9 19.6 %shard_map.47 = f32[4,512,256]{2,1,0:T(8,128)} custom-call(bf16[32,32,256]{2,1,0:T(8,128)(2,1)} %feat_hbm.1, bf16[128,256]{1,0:T(8,128)(2,1)S(1)} %get-tuple-element.18.coarse_ref, bf16[512,256]{1,0:T(8,128)(2,1)S(1)} %get-tuple-element.21.fine_ref, s32[2,2,256]{2,1,0:T(2,128)S(1)} %copy-done), custom_call_target="tpu_custom_call" | custom-call | tf_op jit(solution)/shard_map/pallas_call | solution.py:459
  (1 shorter events, 0.0 us)
Async XLA Ops:
  0.0 0.7 %copy-start.1 = (bf16[1,256]{1,0:T(2,128)(2,1)S(1)}, bf16[1,256]{1,0:T(2,128)(2,1)}, u32[]{:S(2)}) copy-start(bf16[1,256]{1,0:T(2,128)(2,1)} %coarse_hbm.1) | copy-start | bytes 1540
  23.2 0.7 %copy-start = (s32[2,2,256]{2,1,0:T(2,128)S(1)}, s32[2,2,256]{2,1,0:T(2,128)}, u32[]{:S(2)}) copy-start(s32[2,2,256]{2,1,0:T(2,128)} %own_hbm.1) | copy-start | bytes 12292

commit v7 on v6

--- a/solution.py
+++ b/solution.py
@@ -246,7 +246,7 @@
 OFFS = ((-1, -1), (-1, 1), (1, -1), (1, 1), (-1, 0), (0, -1), (0, 1), (1, 0))
 BACK = (3, 2, 1, 0, 7, 6, 5, 4)
 SIDE = 4
-CAPS = tuple(112 if 0 in o else 96 for o in OFFS)
+CAPS = tuple(112 if 0 in o else 80 for o in OFFS)
 STARTS = tuple(sum(CAPS[:n]) for n in range(9))
 
 

time: 44 us -> 43.5 us (0.989)
  Pallas kernels: 42.2 us -> 41.7 us
    pallas_call x1, Pallas kernels: 22.5 us -> 22.1 us  [exchange(): pl.pallas_call(comm_kernel, out_shape=(jax.ShapeDtypeStruct((asked, width...]
where the time goes in v7:
time: 43.5 us; the launch traced here: 43.3 us
  Pallas kernels  41.7 us (96%)
  local copies, waits for them, and re-layouts  1.35 us (3%)
    pallas_call x1, Pallas kernels, exchange(): pl.pallas_call(comm_kernel, out_shape=(jax.ShapeDtypeStruct((asked, width...  22.1 us
    pallas_call x1, Pallas kernels, body(): pl.pallas_call(kernel, out_shape=jax.ShapeDtypeStruct((4, 512, 256), F32)...  19.6 us
    unnamed x4, local copies, waits for them, and re-layouts  1.35 us

profile of v7, /device:TPU:1, one launch (start us, length us, event | category | flops | bytes accessed | tf_op | source)
XLA Modules:
  0.0 43.3 jit_solution(8048509336727232554)
XLA Ops:
  0.0 0.0 copy-start.1
  0.0 0.7 %copy-done.1 = bf16[1,256]{1,0:T(2,128)(2,1)S(1)} copy-done((bf16[1,256]{1,0:T(2,128)(2,1)S(1)}, bf16[1,256]{1,0:T(2,128)(2,1)}, u32[]{:S(2)}) %copy-start.1) | copy-done | bytes 536
  0.7 22.1 %shard_map.46 = (bf16[512,256]{1,0:T(8,128)(2,1)S(1)}, bf16[128,256]{1,0:T(8,128)(2,1)S(1)}, f32[1,128]{1,0:T(1,128)S(1)}) custom-call(bf16[32,32,256]{2,1,0:T(8,128)(2,1)} %feat_hbm.1, bf16[1,256]{1,0:T(2,128)(2,1)S(1)} %copy-done.1, s32[4,128]{1,0:T(4,128)} %bitcast.12), custom_call_target="tpu_custom_call" | custom-call | tf_op jit(solution)/shard_map/pallas_call | solution.py:391
  22.8 0.0 copy-start
  22.8 0.7 %copy-done = s32[2,2,256]{2,1,0:T(2,128)S(1)} copy-done((s32[2,2,256]{2,1,0:T(2,128)S(1)}, s32[2,2,256]{2,1,0:T(2,128)}, u32[]{:S(2)}) %copy-start) | copy-done | bytes 4120
  23.5 19.6 %shard_map.47 = f32[4,512,256]{2,1,0:T(8,128)} custom-call(bf16[32,32,256]{2,1,0:T(8,128)(2,1)} %feat_hbm.1, bf16[128,256]{1,0:T(8,128)(2,1)S(1)} %get-tuple-element.18.coarse_ref, bf16[512,256]{1,0:T(8,128)(2,1)S(1)} %get-tuple-element.21.fine_ref, s32[2,2,256]{2,1,0:T(2,128)S(1)} %copy-done), custom_call_target="tpu_custom_call" | custom-call | tf_op jit(solution)/shard_map/pallas_call | solution.py:459
  (1 shorter events, 0.0 us)
Async XLA Ops:
  0.0 0.7 %copy-start.1 = (bf16[1,256]{1,0:T(2,128)(2,1)S(1)}, bf16[1,256]{1,0:T(2,128)(2,1)}, u32[]{:S(2)}) copy-start(bf16[1,256]{1,0:T(2,128)(2,1)} %coarse_hbm.1) | copy-start | bytes 1540
  22.8 0.7 %copy-start = (s32[2,2,256]{2,1,0:T(2,128)S(1)}, s32[2,2,256]{2,1,0:T(2,128)}, u32[]{:S(2)}) copy-start(s32[2,2,256]{2,1,0:T(2,128)} %own_hbm.1) | copy-start | bytes 12292
